TPU v7x, 256 devices: a whole 4x4x8 slice. The times are simulated.
256 devices in a mesh: gx: 8 (over x, y_hi), gy: 4 (over y_lo, core), gz: 8 (over z).
Axes of the slice: x: 4, y: 4 (y_hi: 2, y_lo: 2; y = y_hi * 2 + y_lo), z: 8, core: 2. Of those that a mesh axis runs over, the one named last changes fastest.
Arguments:
- features: bfloat16 [32, 32, 256, 1024], P(None, 'gx', 'gy', 'gz'), may hold values from -6 to 6
- conv_weight: bfloat16 [27, 32], replicated, may hold values from -0.21875 to 0.21875
- mask: int32 [32, 256, 1024], P('gx', 'gy', 'gz'), may hold values from 0 to 1, as said below
Outputs:
- score: float32 [32, 256, 1024], P('gx', 'gy', 'gz')
- depth: float32 [32, 256, 1024], P('gx', 'gy', 'gz')
Inputs may be any that keep to these rules, and one draw needn't show every extreme that they name: `mask`: 1 marks a foreground voxel and 0 a background voxel; every draw holds both.
All inputs are finite; a program needn't handle non-finite values.
Results may differ from a plain program's by a relative error of at most 0.0003.
Values may be sent and summed in bfloat16 or wider, within the bound.
A program may use at most 128 MiB of HBM per device.

v0:
```python
import functools

import jax
import jax.numpy as jnp
from jax import lax
from jax.experimental import pallas as pl
from jax.experimental.pallas import tpu as pltpu
from jax.sharding import PartitionSpec as P

MESH = pl.DeviceIdType.MESH
RADIUS = 128
CEILING = float(RADIUS * RADIUS)
FAR = 1.0e9
F32 = jnp.float32
BX, BY, BZ = 4, 64, 128
NI, NJ, NK = 8, 4, 8
PLANES = BX + 2
STEPS = RADIUS - 1


def iota(shape, axis):
    return lax.broadcasted_iota(jnp.int32, shape, axis)


def banded_weights(w_ref, wb_ref):
    rows, cols = 9 * 32, 32 * 16
    weights = w_ref[...]
    row = iota((rows, 27), 0)
    tap = iota((rows, 27), 1)
    group = row // 32
    spread = (iota((32, cols), 1) // 16 == iota((32, cols), 0)).astype(jnp.bfloat16)
    gap = iota((rows, cols), 1) % 16 - (iota((rows, cols), 0) % 32 - 8)
    total = jnp.zeros((rows, cols), F32)
    for b in range(3):
        pick = (tap == (group // 3) * 9 + 3 * b + group % 3).astype(jnp.bfloat16)
        own = jnp.dot(pick, weights, preferred_element_type=F32).astype(jnp.bfloat16)
        wide = jnp.dot(own, spread, preferred_element_type=F32)
        total = jnp.where(gap == b - 1, wide, total)
    wb_ref[...] = total.astype(jnp.bfloat16)


def kernel(
    f_ref, w_ref, m_ref, score_ref, depth_ref,
    wb, s3, s, pack, r0, r1, mr, sc, scb, xin, xo, yb, yp, yo, zb, tz,
    r0_send, r0_recv, m_send, m_recv, r1_send, r1_recv, sc_send, sc_recv,
    r2_send, r2_recv, r3_send, r3_recv,
):
    i, j, k = lax.axis_index("gx"), lax.axis_index("gy"), lax.axis_index("gz")

    barrier = pltpu.get_barrier_semaphore()

    def greet(di, dj, dk):
        pl.semaphore_signal(
            barrier, inc=1, device_id=((i + di) % NI, (j + dj) % NJ, (k + dk) % NK), device_id_type=MESH
        )

    greeted = 0
    for di in range(NI):
        for dj in range(NJ):
            if di or dj:
                greet(di, dj, 0)
                greeted += 1
    for dk in (1, NK - 1):
        for dj in range(NJ):
            greet(0, dj, dk)
            greeted += 1

    banded_weights(w_ref, wb)
    s3[...] = jnp.zeros_like(s3)

    def conv_block(q, carry):
        start = pl.multiple_of(q * 16, 16)
        for xs in range(BX):
            block = f_ref[:, xs, pl.ds(start, 16), :].reshape(32 * 16, BZ)
            part = jnp.dot(wb[...], block, preferred_element_type=F32)
            for a in range(3):
                for c in range(3):
                    at = (3 * a + c) * 32
                    s3[c, xs - a + 2, pl.ds(start, 32), :] += part[at : at + 32]
        return carry

    lax.fori_loop(0, BY // 16, conv_block, 0)

    lane = iota((8, BZ), 1)
    sub = iota((8, BZ), 0)
    edge = (lane == 0) | (lane == BZ - 1)
    pack[...] = jnp.zeros_like(pack)

    def shift_plane(p, tile):
        for t in range(10):
            rows = pl.ds(8 * t, 8)
            right = pltpu.roll(s3[0, p, rows, :], 1, 1)
            left = pltpu.roll(s3[2, p, rows, :], BZ - 1, 1)
            mine = s3[1, p, rows, :] + jnp.where(lane == 0, 0.0, right) + jnp.where(lane == BZ - 1, 0.0, left)
            s[p, rows, :] = mine
            rim = jnp.where(lane == 0, right, left)
            if t == 0:
                pack[1, pl.ds(p, 1), :] = mine[7:8]
                pack[2, pl.ds(p, 1), :] = rim[7:8]
            elif t == 9:
                pack[3, pl.ds(p, 1), :] = mine[0:1]
                pack[4, pl.ds(p, 1), :] = rim[0:1]
            else:
                v = 2 * (p * 8 + t - 1)
                moved = pltpu.roll(rim, v, 1)
                tile = jnp.where((lane == v) | (lane == (v + BZ - 1) % BZ), moved, tile)
        return tile

    pack[0] = lax.fori_loop(0, PLANES, shift_plane, jnp.zeros((8, BZ), F32))

    pl.semaphore_wait(barrier, greeted)

    def mask_rows(step, carry):
        to = (i + step) % NI
        pltpu.make_async_remote_copy(
            m_ref.at[:, pl.ds(pl.multiple_of(to * 8, 8), 8), :], mr.at[i], m_send, m_recv,
            device_id=(to, j, k), device_id_type=MESH,
        ).start()
        return carry

    slot = 0
    halo = []
    for dj, dk, source in (
        (0, 1, 0), (0, -1, 0), (-1, 0, 1), (-1, 1, 2), (-1, -1, 2), (1, 0, 3), (1, 1, 4), (1, -1, 4)
    ):
        copy = pltpu.make_async_remote_copy(
            pack.at[source], r0.at[slot], r0_send.at[slot], r0_recv.at[slot],
            device_id=(i, (j + dj) % NJ, (k + dk) % NK), device_id_type=MESH,
        )
        copy.start()
        halo.append(copy)
        slot += 1
    lax.fori_loop(1, NI, mask_rows, 0)
    pltpu.make_async_copy(m_ref.at[:, pl.ds(pl.multiple_of(i * 8, 8), 8), :], mr.at[i], m_recv).start()
    for copy in halo:
        copy.wait()

    first_z, last_z, first_y, last_y = k == 0, k == NK - 1, j == 0, j == NJ - 1
    zero = jnp.zeros((8, BZ), F32)

    def unless(absent, value):
        return jnp.where(absent, zero, value)

    lower, upper = unless(first_z, r0[0]), unless(last_z, r0[1])
    both = jnp.where(lane % 2 == 0, lower, upper)
    below = r0[2] + jnp.where(lane == 0, unless(first_z, r0[3]), 0.0)
    below = unless(last_y, below + jnp.where(lane == BZ - 1, unless(last_z, r0[4]), 0.0))
    above = r0[5] + jnp.where(lane == 0, unless(first_z, r0[6]), 0.0)
    above = unless(first_y, above + jnp.where(lane == BZ - 1, unless(last_z, r0[7]), 0.0))
    pack[1] = below
    pack[2] = above

    def add_halo(p, carry):
        for t in range(1, 9):
            rows = pl.ds(8 * t, 8)
            v = 2 * (p * 8 + t - 1)
            moved = pltpu.roll(both, (2 * BZ - v) % BZ, 1)
            value = s[p, rows, :] + jnp.where(edge, moved, 0.0)
            if t == 1:
                value += jnp.where(sub == 0, pack[2, pl.ds(p, 1), :], 0.0)
            if t == 8:
                value += jnp.where(sub == 7, pack[1, pl.ds(p, 1), :], 0.0)
            s[p, rows, :] = value
        return carry

    lax.fori_loop(0, PLANES, add_halo, 0)

    def part_rows(to):
        return s.at[:, pl.ds(pl.multiple_of(8 + to * 8, 8), 8), :]

    def send_parts(step, carry):
        to = (i + step) % NI
        pltpu.make_async_remote_copy(
            part_rows(to), r1.at[i], r1_send, r1_recv, device_id=(to, j, k), device_id_type=MESH
        ).start()
        return carry

    lax.fori_loop(1, NI, send_parts, 0)
    pltpu.make_async_copy(part_rows(i), r1.at[i], r1_recv).start()
    pltpu.make_async_copy(r1, r1, r1_recv).wait()
    pltpu.make_async_copy(mr, mr, m_recv).wait()

    for b in range(NI):
        for a in range(BX):
            value = r1[b, a + 1]
            if a == 0 and b > 0:
                value += r1[b - 1, BX + 1]
            if a == BX - 1 and b < NI - 1:
                value += r1[b + 1, 0]
            x = BX * b + a
            sc[x] = value
            cost = CEILING / (1.0 + jnp.exp(-value))
            xin[32 + x] = jnp.where(mr[b, a] == 1, CEILING, cost)

    def send_scores(step, carry):
        to = (i + step) % NI
        pltpu.make_async_remote_copy(
            sc.at[pl.ds(to * BX, BX)], scb.at[i], sc_send, sc_recv, device_id=(to, j, k), device_id_type=MESH
        ).start()
        return carry

    lax.fori_loop(1, NI, send_scores, 0)
    pltpu.make_async_copy(sc.at[pl.ds(i * BX, BX)], scb.at[i], sc_recv).start()

    far = jnp.full((32, 8, BZ), FAR, F32)
    xin[0:32] = far
    xin[64:96] = far

    def step_x(n, acc):
        square = (n * n).astype(F32)
        return jnp.minimum(acc, jnp.minimum(xin[pl.ds(32 - n, 32)], xin[pl.ds(32 + n, 32)]) + square)

    xo[...] = lax.fori_loop(1, 32, step_x, xin[32:64])

    def send_x(step, carry):
        peer = (i * NJ + j + step) % (NI * NJ)
        ti, tj = peer // NJ, peer % NJ
        pltpu.make_async_remote_copy(
            xo.at[peer], yb.at[j * NI + i], r2_send, r2_recv, device_id=(ti, tj, k), device_id_type=MESH
        ).start()
        return carry

    lax.fori_loop(1, NI * NJ, send_x, 0)
    pltpu.make_async_copy(xo.at[i * NJ + j], yb.at[j * NI + i], r2_recv).start()

    edge_rows = jnp.full((128, BZ), FAR, F32)
    yp[0:128] = edge_rows
    yp[384:512] = edge_rows
    pltpu.make_async_copy(yb, yb, r2_recv).wait()
    yp[128:384] = yb[...].reshape(256, BZ)

    def step_y(n, acc):
        square = (n * n).astype(F32)
        low = yp[pl.ds(128 - n, 256), :]
        high = yp[pl.ds(128 + n, 256), :]
        return jnp.minimum(acc, jnp.minimum(low, high) + square)

    yo[...] = lax.fori_loop(1, STEPS + 1, step_y, yp[128:384])

    def y_rows(to):
        return yo.at[pl.ds(pl.multiple_of(to * BY, BY), BY), :]

    for dj in range(NJ):
        for dk in (1, -1, 0):
            to = (j + dj) % NJ
            if dj == 0 and dk == 0:
                pltpu.make_async_copy(y_rows(to), zb.at[NJ + j], r3_recv).start()
            else:
                pltpu.make_async_remote_copy(
                    y_rows(to), zb.at[NJ * (1 - dk) + j], r3_send, r3_recv,
                    device_id=(i, to, (k + dk) % NK), device_id_type=MESH,
                ).start()
    pltpu.make_async_copy(zb, zb, r3_recv).wait()

    for d in range(3):
        for h in range(2):
            turned = zb[NJ * d + 2 * h : NJ * d + 2 * h + 2].reshape(128, BZ).T
            if d == 0:
                turned = jnp.where(first_z, FAR, turned)
            if d == 2:
                turned = jnp.where(last_z, FAR, turned)
            tz[h, 128 * d : 128 * d + 128, :] = turned

    def step_z(n, acc):
        square = (n * n).astype(F32)
        low = tz[:, pl.ds(128 - n, 128), :]
        high = tz[:, pl.ds(128 + n, 128), :]
        return jnp.minimum(acc, jnp.minimum(low, high) + square)

    least = lax.fori_loop(1, STEPS + 1, step_z, tz[:, 128:256, :])
    for h in range(2):
        depth_ref[2 * h : 2 * h + 2] = (least[h] * (1.0 / RADIUS)).T.reshape(2, BY, BZ)

    pltpu.make_async_copy(scb, scb, sc_recv).wait()
    for b in range(NI):
        score_ref[:, 8 * b : 8 * b + 8, :] = scb[b]

    seven = pl.ds(0, NI - 1)
    pltpu.make_async_copy(mr.at[seven], mr.at[seven], m_send).wait()
    pltpu.make_async_copy(r1.at[seven], r1.at[seven], r1_send).wait()
    pltpu.make_async_copy(scb.at[seven], scb.at[seven], sc_send).wait()
    most = pl.ds(0, NI * NJ - 1)
    pltpu.make_async_copy(yb.at[most], yb.at[most], r2_send).wait()
    most = pl.ds(0, 3 * NJ - 1)
    pltpu.make_async_copy(zb.at[most], zb.at[most], r3_send).wait()


def shards(features, conv_weight, mask):
    vmem = pl.BlockSpec(memory_space=pltpu.VMEM)
    tile = (8, BZ)
    dma = pltpu.SemaphoreType.DMA
    out = jax.ShapeDtypeStruct((BX, BY, BZ), F32)
    return pl.pallas_call(
        kernel,
        out_shape=(out, out),
        in_specs=[vmem] * 3,
        out_specs=(vmem, vmem),
        scratch_shapes=[
            pltpu.VMEM((288, 512), jnp.bfloat16),
            pltpu.VMEM((3, PLANES, BY + 16, BZ), F32),
            pltpu.VMEM((PLANES, BY + 16, BZ), F32),
            pltpu.VMEM((5, *tile), F32),
            pltpu.VMEM((8, *tile), F32),
            pltpu.VMEM((NI, PLANES, *tile), F32),
            pltpu.VMEM((NI, BX, *tile), jnp.int32),
            pltpu.VMEM((32, *tile), F32),
            pltpu.VMEM((NI, BX, *tile), F32),
            pltpu.VMEM((96, *tile), F32),
            pltpu.VMEM((32, *tile), F32),
            pltpu.VMEM((32, *tile), F32),
            pltpu.VMEM((512, BZ), F32),
            pltpu.VMEM((256, BZ), F32),
            pltpu.VMEM((3 * NJ, BY, BZ), F32),
            pltpu.VMEM((2, 384, BZ), F32),
            dma((8,)), dma((8,)),
        ] + [dma] * 10,
        compiler_params=pltpu.CompilerParams(
            collective_id=0, has_side_effects=True, vmem_limit_bytes=40 * 1024 * 1024
        ),
    )(features, conv_weight, mask)


def solution(mesh):
    in_specs = (P(None, "gx", "gy", "gz"), P(), P("gx", "gy", "gz"))
    out_specs = (P("gx", "gy", "gz"), P("gx", "gy", "gz"))
    return jax.shard_map(shards, mesh=mesh, in_specs=in_specs, out_specs=out_specs, check_vma=False)
```

profile of v0, /device:TPU:1, one launch (start us, length us, event | category | flops | bytes accessed | tf_op | source)
XLA Modules:
  0.0 47.3 jit_solution(6111717182335449999)
XLA Ops:
  0.6 0.0 copy-start
  0.6 1.6 %copy-done = bf16[32,4,64,128]{3,2,1,0:T(8,128)(2,1)S(1)} copy-done((bf16[32,4,64,128]{3,2,1,0:T(8,128)(2,1)S(1)}, bf16[32,4,64,128]{3,2,1,0:T(8,128)(2,1)}, u32[]{:S(2)}) %copy-start) | copy-done | bytes 2097176
  2.2 0.0 copy-start.1
  2.2 0.9 %copy-done.1 = s32[4,64,128]{2,1,0:T(8,128)S(1)} copy-done((s32[4,64,128]{2,1,0:T(8,128)S(1)}, s32[4,64,128]{2,1,0:T(8,128)}, u32[]{:S(2)}) %copy-start.1) | copy-done | bytes 131096
  3.1 0.0 copy-start.2
  3.1 0.7 %copy-done.2 = bf16[27,32]{1,0:T(8,128)(2,1)S(1)} copy-done((bf16[27,32]{1,0:T(8,128)(2,1)S(1)}, bf16[27,32]{1,0:T(8,128)(2,1)}, u32[]{:S(2)}) %copy-start.2) | copy-done | bytes 1752
  3.8 42.2 %shard_map.50 = (f32[4,64,128]{2,1,0:T(8,128)S(1)}, f32[4,64,128]{2,1,0:T(8,128)S(1)}) custom-call(bf16[32,4,64,128]{3,2,1,0:T(8,128)(2,1)S(1)} %copy-done, bf16[27,32]{1,0:T(8,128)(2,1)S(1)} %copy-done.2, s32[4,64,128]{2,1,0:T(8,128)S(1)} %copy-done.1), custom_call_target="tpu_custom_call" | custom-call | tf_op jit(solution)/shard_map/pallas_call | solution.py:293
  46.0 0.7 %copy.7 = f32[4,64,128]{2,1,0:T(8,128)} copy(f32[4,64,128]{2,1,0:T(8,128)S(1)} %get-tuple-element.4) | data formatting | bytes 262144
  46.7 0.7 %copy.8 = f32[4,64,128]{2,1,0:T(8,128)} copy(f32[4,64,128]{2,1,0:T(8,128)S(1)} %get-tuple-element.5) | data formatting | bytes 262144
Async XLA Ops:
  0.6 1.6 %copy-start = (bf16[32,4,64,128]{3,2,1,0:T(8,128)(2,1)S(1)}, bf16[32,4,64,128]{3,2,1,0:T(8,128)(2,1)}, u32[]{:S(2)}) copy-start(bf16[32,4,64,128]{3,2,1,0:T(8,128)(2,1)} %f_ref.1) | copy-start | bytes 6291460
  2.2 0.9 %copy-start.1 = (s32[4,64,128]{2,1,0:T(8,128)S(1)}, s32[4,64,128]{2,1,0:T(8,128)}, u32[]{:S(2)}) copy-start(s32[4,64,128]{2,1,0:T(8,128)} %m_ref.1) | copy-start | bytes 393220
  3.1 0.7 %copy-start.2 = (bf16[27,32]{1,0:T(8,128)(2,1)S(1)}, bf16[27,32]{1,0:T(8,128)(2,1)}, u32[]{:S(2)}) copy-start(bf16[27,32]{1,0:T(8,128)(2,1)} %w_ref.1) | copy-start | bytes 5188
where the time goes:
time: 47.5 us; the launch traced here: 47.3 us
  Pallas kernels  42.2 us (89%)
  local copies, waits for them, and re-layouts  4.5 us (9%)
  between operations  0.65 us (1%)
    pallas_call x1, Pallas kernels, shards(): pl.pallas_call(kernel, out_shape=(out, out), in_specs=[vmem] * 3, out_spe...  42.2 us
    unnamed x8, local copies, waits for them, and re-layouts  4.5 us

commit v1 on v0

v1 whole, which is shorter than its diff:
```python
import functools

import jax
import jax.numpy as jnp
from jax import lax
from jax.experimental import pallas as pl
from jax.experimental.pallas import tpu as pltpu
from jax.sharding import PartitionSpec as P

MESH = pl.DeviceIdType.MESH
RADIUS = 128
CEILING = float(RADIUS * RADIUS)
FAR = 1.0e9
F32 = jnp.float32
BX, BY, BZ = 4, 64, 128
NI, NJ, NK = 8, 4, 8
PLANES = BX + 2
STEPS = RADIUS - 1


def iota(shape, axis):
    return lax.broadcasted_iota(jnp.int32, shape, axis)


def banded_weights(w_ref, wb_ref):
    rows, cols = 9 * 32, 32 * 16
    weights = w_ref[...]
    row = iota((rows, 27), 0)
    tap = iota((rows, 27), 1)
    group = row // 32
    spread = (iota((32, cols), 1) // 16 == iota((32, cols), 0)).astype(jnp.bfloat16)
    gap = iota((rows, cols), 1) % 16 - (iota((rows, cols), 0) % 32 - 8)
    total = jnp.zeros((rows, cols), F32)
    for b in range(3):
        pick = (tap == (group // 3) * 9 + 3 * b + group % 3).astype(jnp.bfloat16)
        own = jnp.dot(pick, weights, preferred_element_type=F32).astype(jnp.bfloat16)
        wide = jnp.dot(own, spread, preferred_element_type=F32)
        total = jnp.where(gap == b - 1, wide, total)
    wb_ref[...] = total.astype(jnp.bfloat16)


def kernel(
    f_hbm, w_hbm, m_hbm, score_ref, depth_ref,
    f_ref, w_ref, m_ref, wb, s3, s, pack, r1, rims, rows_in, mr, sc, scb, xin, xo, yb, yp, yo, zb, tz,
    in_sems, m_send, m_recv, r1_send, r1_recv, t_send, t_recv, row_send, row_recv, sc_send, sc_recv,
    r2_send, r2_recv, r3_send, r3_recv,
):
    i, j, k = lax.axis_index("gx"), lax.axis_index("gy"), lax.axis_index("gz")
    loads = [
        pltpu.make_async_copy(source, target, in_sems.at[n])
        for n, (source, target) in enumerate(((w_hbm, w_ref), (f_hbm, f_ref), (m_hbm, m_ref)))
    ]
    for load in loads:
        load.start()

    barrier = pltpu.get_barrier_semaphore()

    def greet(di, dj, dk):
        pl.semaphore_signal(
            barrier, inc=1, device_id=((i + di) % NI, (j + dj) % NJ, (k + dk) % NK), device_id_type=MESH
        )

    def greet_plane(step, carry):
        greet(step // NJ, step % NJ, 0)
        return carry

    def greet_sides(step, carry):
        greet(step % NI, 0, 1)
        greet(step % NI, 0, NK - 1)
        return carry

    def greet_lines(step, carry):
        greet(0, step, 1)
        greet(0, step, NK - 1)
        return carry

    lax.fori_loop(1, NI * NJ, greet_plane, 0)
    lax.fori_loop(0, NI, greet_sides, 0)
    lax.fori_loop(1, NJ, greet_lines, 0)
    at_end = (i == 0) | (i == NI - 1)

    @pl.when(at_end)
    def _():
        dj = jnp.where(i == 0, NJ - 1, 1)

        def greet_corners(step, carry):
            greet(step, dj, 1)
            greet(step, dj, NK - 1)
            return carry

        lax.fori_loop(0, NI, greet_corners, 0)

    greeted = NI * NJ - 1 + 2 * NI + 2 * (NJ - 1) + 4

    loads[0].wait()
    banded_weights(w_ref, wb)
    s3[...] = jnp.zeros_like(s3)
    loads[1].wait()

    def conv_block(q, carry):
        start = pl.multiple_of(q * 16, 16)
        for xs in range(BX):
            block = f_ref[:, xs, pl.ds(start, 16), :].reshape(32 * 16, BZ)
            part = jnp.dot(wb[...], block, preferred_element_type=F32)
            for a in range(3):
                for c in range(3):
                    at = (3 * a + c) * 32
                    s3[c, xs - a + 2, pl.ds(start, 32), :] += part[at : at + 32]
        return carry

    lax.fori_loop(0, BY // 16, conv_block, 0)

    lane = iota((8, BZ), 1)
    sub = iota((8, BZ), 0)
    edge = (lane == 0) | (lane == BZ - 1)
    zero = jnp.zeros((8, BZ), F32)
    pack[...] = jnp.zeros_like(pack)

    def shift_plane(p, tile):
        for t in range(10):
            rows = pl.ds(8 * t, 8)
            right = pltpu.roll(s3[0, p, rows, :], 1, 1)
            left = pltpu.roll(s3[2, p, rows, :], BZ - 1, 1)
            mine = s3[1, p, rows, :] + jnp.where(lane == 0, 0.0, right) + jnp.where(lane == BZ - 1, 0.0, left)
            s[p, rows, :] = mine
            rim = jnp.where(lane == 0, right, left)
            if t == 0:
                pack[1, pl.ds(p, 1), :] = mine[7:8]
                pack[2, pl.ds(p, 1), :] = rim[7:8]
            elif t == 9:
                pack[3, pl.ds(p, 1), :] = mine[0:1]
                pack[4, pl.ds(p, 1), :] = rim[0:1]
            else:
                v = 2 * (p * 8 + t - 1)
                moved = pltpu.roll(rim, v, 1)
                tile = jnp.where((lane == v) | (lane == (v + BZ - 1) % BZ), moved, tile)
        return tile

    pack[0] = lax.fori_loop(0, PLANES, shift_plane, zero)
    far = jnp.full((128, BZ), FAR, F32)
    yp[0:128] = far
    yp[384:512] = far

    @pl.when(jnp.logical_not(at_end))
    def _():
        rows_in[...] = jnp.zeros_like(rows_in)

    loads[2].wait()
    pl.semaphore_wait(barrier, greeted)

    def part_rows(to):
        return s.at[:, pl.ds(pl.multiple_of(8 + to * 8, 8), 8), :]

    def mask_rows(to):
        return m_ref.at[:, pl.ds(pl.multiple_of(to * 8, 8), 8), :]

    def remote(source, target, send, recv, device):
        pltpu.make_async_remote_copy(
            source, target, send, recv, device_id=device, device_id_type=MESH
        ).start()

    def send_parts(step, carry):
        to = (i + step) % NI
        remote(part_rows(to), r1.at[i], r1_send, r1_recv, (to, j, k))
        remote(pack.at[0], rims.at[i], t_send, t_recv, (to, j, (k + 1) % NK))
        remote(pack.at[0], rims.at[NI + i], t_send, t_recv, (to, j, (k + NK - 1) % NK))
        remote(mask_rows(to), mr.at[i], m_send, m_recv, (to, j, k))
        return carry

    for ti, dj, near in ((NI - 1, -1, 1), (0, 1, 3)):
        tj = (j + dj) % NJ
        remote(pack.at[near + 1], rows_in.at[NI + i], row_send, row_recv, (ti, tj, (k + 1) % NK))
        remote(pack.at[near + 1], rows_in.at[2 * NI + i], row_send, row_recv, (ti, tj, (k + NK - 1) % NK))
        remote(pack.at[near], rows_in.at[i], row_send, row_recv, (ti, tj, k))
    lax.fori_loop(1, NI, send_parts, 0)
    remote(pack.at[0], rims.at[i], t_send, t_recv, (i, j, (k + 1) % NK))
    remote(pack.at[0], rims.at[NI + i], t_send, t_recv, (i, j, (k + NK - 1) % NK))
    pltpu.make_async_copy(part_rows(i), r1.at[i], r1_recv).start()
    pltpu.make_async_copy(mask_rows(i), mr.at[i], m_recv).start()

    first_z, last_z = k == 0, k == NK - 1
    outside = ((i == 0) & (j == 0)) | ((i == NI - 1) & (j == NJ - 1))

    def drain(ref, semaphore):
        pltpu.make_async_copy(ref, ref, semaphore).wait()

    @pl.when(at_end)
    def _():
        drain(rows_in, row_recv)

    drain(r1, r1_recv)
    drain(rims, t_recv)
    drain(mr, m_recv)

    end_row = sub == jnp.where(i == 0, 0, 7)
    parts = []
    for b in range(NI):
        both = jnp.where(
            lane % 2 == 0, jnp.where(first_z, zero, rims[b]), jnp.where(last_z, zero, rims[NI + b])
        )
        both = pltpu.roll(both, (2 * BZ - 2 * i) % BZ, 1)
        rows = rows_in[b] + jnp.where((lane == 0) & jnp.logical_not(first_z), rows_in[NI + b], 0.0)
        rows += jnp.where((lane == BZ - 1) & jnp.logical_not(last_z), rows_in[2 * NI + b], 0.0)
        rows = jnp.where(outside, zero, rows)
        planes = []
        for p in range(PLANES):
            moved = both if p == 0 else pltpu.roll(both, BZ - 16 * p, 1)
            planes.append(
                r1[b, p]
                + jnp.where(edge, moved, 0.0)
                + jnp.where(end_row, jnp.broadcast_to(rows[p : p + 1], (8, BZ)), 0.0)
            )
        parts.append(planes)
    for b in range(NI):
        for a in range(BX):
            value = parts[b][a + 1]
            if a == 0 and b > 0:
                value += parts[b - 1][BX + 1]
            if a == BX - 1 and b < NI - 1:
                value += parts[b + 1][0]
            x = BX * b + a
            sc[x] = value
            cost = CEILING / (1.0 + jnp.exp(-value))
            xin[x] = jnp.where(mr[b, a] == 1, CEILING, cost)

    acc = xin[...]
    for n in range(1, 32):
        square = float(n * n)
        if n < 16:
            pair = jnp.minimum(xin[0 : 32 - 2 * n], xin[2 * n : 32]) + square
            least = jnp.concatenate([xin[n : 2 * n] + square, pair, xin[32 - 2 * n : 32 - n] + square], axis=0)
            acc = jnp.minimum(acc, least)
        else:
            low = jnp.minimum(acc[0 : 32 - n], xin[n:32] + square)
            high = jnp.minimum(acc[n:32], xin[0 : 32 - n] + square)
            middle = [acc[32 - n : n]] if n > 16 else []
            acc = jnp.concatenate([low, *middle, high], axis=0)
    xo[...] = acc

    def send_x(step, carry):
        peer = (i * NJ + j + step) % (NI * NJ)
        remote(xo.at[peer], yb.at[j * NI + i], r2_send, r2_recv, (peer // NJ, peer % NJ, k))
        return carry

    lax.fori_loop(1, NI * NJ, send_x, 0)
    pltpu.make_async_copy(xo.at[i * NJ + j], yb.at[j * NI + i], r2_recv).start()

    def send_scores(step, carry):
        to = (i + step) % NI
        remote(sc.at[pl.ds(to * BX, BX)], scb.at[i], sc_send, sc_recv, (to, j, k))
        return carry

    lax.fori_loop(1, NI, send_scores, 0)
    pltpu.make_async_copy(sc.at[pl.ds(i * BX, BX)], scb.at[i], sc_recv).start()

    drain(yb, r2_recv)
    yp[128:384] = yb[...].reshape(256, BZ)

    for turn, to in enumerate(((j + 2) % NJ, NJ - 1 - j, j + 1 - 2 * (j % 2), j)):
        base = pl.multiple_of(128 + to * BY, BY)

        def step_y(n, acc):
            square = (n * n).astype(F32)
            low = yp[pl.ds(base - n, BY), :]
            high = yp[pl.ds(base + n, BY), :]
            return jnp.minimum(acc, jnp.minimum(low, high) + square)

        yo[turn] = lax.fori_loop(1, STEPS + 2, step_y, yp[pl.ds(base, BY), :], unroll=8)
        for dk in (1, -1, 0):
            if turn == 3 and dk == 0:
                pltpu.make_async_copy(yo.at[turn], zb.at[NJ + j], r3_recv).start()
            else:
                remote(
                    yo.at[turn], zb.at[NJ * (1 - dk) + j], r3_send, r3_recv, (i, to, (k + dk) % NK)
                )

    drain(scb, sc_recv)
    for b in range(NI):
        score_ref[:, 8 * b : 8 * b + 8, :] = scb[b]
    drain(zb, r3_recv)

    for h in range(2):
        for d in range(3):
            turned = zb[NJ * d + 2 * h : NJ * d + 2 * h + 2].reshape(128, BZ).T
            if d == 0:
                turned = jnp.where(first_z, FAR, turned)
            if d == 2:
                turned = jnp.where(last_z, FAR, turned)
            tz[h, 128 * d : 128 * d + 128, :] = turned

        def step_z(n, acc):
            square = (n * n).astype(F32)
            low = tz[h, pl.ds(128 - n, 128), :]
            high = tz[h, pl.ds(128 + n, 128), :]
            return jnp.minimum(acc, jnp.minimum(low, high) + square)

        least = lax.fori_loop(1, STEPS + 2, step_z, tz[h, 128:256, :], unroll=4)
        depth_ref[2 * h : 2 * h + 2] = (least * (1.0 / RADIUS)).T.reshape(2, BY, BZ)

    seven = pl.ds(0, NI - 1)
    drain(mr.at[seven], m_send)
    drain(r1.at[seven], r1_send)
    drain(scb.at[seven], sc_send)
    drain(rims, t_send)
    drain(rows_in.at[pl.ds(0, 6)], row_send)
    drain(yb.at[pl.ds(0, NI * NJ - 1)], r2_send)
    drain(zb.at[pl.ds(0, 3 * NJ - 1)], r3_send)


def shards(features, conv_weight, mask):
    vmem = pl.BlockSpec(memory_space=pltpu.VMEM)
    hbm = pl.BlockSpec(memory_space=pltpu.HBM)
    tile = (8, BZ)
    dma = pltpu.SemaphoreType.DMA
    out = jax.ShapeDtypeStruct((BX, BY, BZ), F32)
    return pl.pallas_call(
        kernel,
        out_shape=(out, out),
        in_specs=[hbm] * 3,
        out_specs=(vmem, vmem),
        scratch_shapes=[
            pltpu.VMEM((32, BX, BY, BZ), jnp.bfloat16),
            pltpu.VMEM((27, 32), jnp.bfloat16),
            pltpu.VMEM((BX, BY, BZ), jnp.int32),
            pltpu.VMEM((288, 512), jnp.bfloat16),
            pltpu.VMEM((3, PLANES, BY + 16, BZ), F32),
            pltpu.VMEM((PLANES, BY + 16, BZ), F32),
            pltpu.VMEM((5, *tile), F32),
            pltpu.VMEM((NI, PLANES, *tile), F32),
            pltpu.VMEM((2 * NI, *tile), F32),
            pltpu.VMEM((3 * NI, *tile), F32),
            pltpu.VMEM((NI, BX, *tile), jnp.int32),
            pltpu.VMEM((32, *tile), F32),
            pltpu.VMEM((NI, BX, *tile), F32),
            pltpu.VMEM((32, *tile), F32),
            pltpu.VMEM((32, *tile), F32),
            pltpu.VMEM((32, *tile), F32),
            pltpu.VMEM((512, BZ), F32),
            pltpu.VMEM((NJ, BY, BZ), F32),
            pltpu.VMEM((3 * NJ, BY, BZ), F32),
            pltpu.VMEM((2, 384, BZ), F32),
            dma((3,)),
        ] + [dma] * 14,
        compiler_params=pltpu.CompilerParams(
            collective_id=0, has_side_effects=True, vmem_limit_bytes=40 * 1024 * 1024
        ),
    )(features, conv_weight, mask)


def solution(mesh):
    in_specs = (P(None, "gx", "gy", "gz"), P(), P("gx", "gy", "gz"))
    out_specs = (P("gx", "gy", "gz"), P("gx", "gy", "gz"))
    return jax.shard_map(shards, mesh=mesh, in_specs=in_specs, out_specs=out_specs, check_vma=False)
```

time: 47.5 us -> 41 us (0.86)
  Pallas kernels: 42.2 us -> 35.6 us
    pallas_call x1, Pallas kernels: 42.2 us -> 35.6 us  [shards(): pl.pallas_call(kernel, out_shape=(out, out), in_specs=[hbm] * 3, out_spec...]
where the time goes in v1:
time: 41 us; the launch traced here: 40.8 us
  Pallas kernels  35.6 us (87%)
  local copies, waits for them, and re-layouts  4.5 us (11%)
  between operations  0.65 us (2%)
    pallas_call x1, Pallas kernels, shards(): pl.pallas_call(kernel, out_shape=(out, out), in_specs=[hbm] * 3, out_spec...  35.6 us
    unnamed x8, local copies, waits for them, and re-layouts  4.5 us

profile of v1, /device:TPU:1, one launch (start us, length us, event | category | flops | bytes accessed | tf_op | source)
XLA Modules:
  0.0 40.8 jit_solution(2155727782354123321)
XLA Ops:
  0.6 0.0 copy-start
  0.6 1.6 %copy-done = bf16[32,4,64,128]{3,2,1,0:T(8,128)(2,1)S(1)} copy-done((bf16[32,4,64,128]{3,2,1,0:T(8,128)(2,1)S(1)}, bf16[32,4,64,128]{3,2,1,0:T(8,128)(2,1)}, u32[]{:S(2)}) %copy-start) | copy-done | bytes 2097176
  2.2 0.0 copy-start.1
  2.2 0.9 %copy-done.1 = s32[4,64,128]{2,1,0:T(8,128)S(1)} copy-done((s32[4,64,128]{2,1,0:T(8,128)S(1)}, s32[4,64,128]{2,1,0:T(8,128)}, u32[]{:S(2)}) %copy-start.1) | copy-done | bytes 131096
  3.1 0.0 copy-start.2
  3.1 0.7 %copy-done.2 = bf16[27,32]{1,0:T(8,128)(2,1)S(1)} copy-done((bf16[27,32]{1,0:T(8,128)(2,1)S(1)}, bf16[27,32]{1,0:T(8,128)(2,1)}, u32[]{:S(2)}) %copy-start.2) | copy-done | bytes 1752
  3.8 35.6 %shard_map.50 = (f32[4,64,128]{2,1,0:T(8,128)S(1)}, f32[4,64,128]{2,1,0:T(8,128)S(1)}) custom-call(bf16[32,4,64,128]{3,2,1,0:T(8,128)(2,1)S(1)} %copy-done, bf16[27,32]{1,0:T(8,128)(2,1)S(1)} %copy-done.2, s32[4,64,128]{2,1,0:T(8,128)S(1)} %copy-done.1), custom_call_target="tpu_custom_call" | custom-call | tf_op jit(solution)/shard_map/pallas_call | solution.py:316
  39.5 0.7 %copy.7 = f32[4,64,128]{2,1,0:T(8,128)} copy(f32[4,64,128]{2,1,0:T(8,128)S(1)} %get-tuple-element.4) | data formatting | bytes 262144
  40.1 0.7 %copy.8 = f32[4,64,128]{2,1,0:T(8,128)} copy(f32[4,64,128]{2,1,0:T(8,128)S(1)} %get-tuple-element.5) | data formatting | bytes 262144
Async XLA Ops:
  0.6 1.6 %copy-start = (bf16[32,4,64,128]{3,2,1,0:T(8,128)(2,1)S(1)}, bf16[32,4,64,128]{3,2,1,0:T(8,128)(2,1)}, u32[]{:S(2)}) copy-start(bf16[32,4,64,128]{3,2,1,0:T(8,128)(2,1)} %f_hbm.1) | copy-start | bytes 6291460
  2.2 0.9 %copy-start.1 = (s32[4,64,128]{2,1,0:T(8,128)S(1)}, s32[4,64,128]{2,1,0:T(8,128)}, u32[]{:S(2)}) copy-start(s32[4,64,128]{2,1,0:T(8,128)} %m_hbm.1) | copy-start | bytes 393220
  3.1 0.7 %copy-start.2 = (bf16[27,32]{1,0:T(8,128)(2,1)S(1)}, bf16[27,32]{1,0:T(8,128)(2,1)}, u32[]{:S(2)}) copy-start(bf16[27,32]{1,0:T(8,128)(2,1)} %w_hbm.1) | copy-start | bytes 5188

commit v2 on v1

--- a/solution.py
+++ b/solution.py
@@ -41,9 +41,9 @@
 
 def kernel(
     f_hbm, w_hbm, m_hbm, score_ref, depth_ref,
-    f_ref, w_ref, m_ref, wb, s3, s, pack, r1, rims, rows_in, mr, sc, scb, xin, xo, yb, yp, yo, zb, tz,
-    in_sems, m_send, m_recv, r1_send, r1_recv, t_send, t_recv, row_send, row_recv, sc_send, sc_recv,
-    r2_send, r2_recv, r3_send, r3_recv,
+    f_ref, w_ref, m_ref, wb, s3, s, pack, r1, rims, rims_y, rows_in, mr, sc, scb, xin, xo, yb, yp, yo, zb, tz,
+    in_sems, m_send, m_recv, r1_send, r1_recv, row_send, row_recv, sc_send, sc_recv,
+    r2_send, r2_recv, t_send, t_recv, ry_send, ry_recv, r3_send, r3_recv,
 ):
     i, j, k = lax.axis_index("gx"), lax.axis_index("gy"), lax.axis_index("gz")
     loads = [
@@ -53,44 +53,43 @@
     for load in loads:
         load.start()
 
+    def around(position, size):
+        return [position] + [
+            jnp.where(position >= size - d, position - (size - d), position + d) for d in range(1, size)
+        ]
+
+    xs_of, ys_of = around(i, NI), around(j, NJ)
+    first_z, last_z = k == 0, k == NK - 1
+    sides = ((1, k + 1, jnp.logical_not(last_z)), (0, k - 1, jnp.logical_not(first_z)))
+    side_count = 2 - first_z.astype(jnp.int32) - last_z.astype(jnp.int32)
+
     barrier = pltpu.get_barrier_semaphore()
 
-    def greet(di, dj, dk):
-        pl.semaphore_signal(
-            barrier, inc=1, device_id=((i + di) % NI, (j + dj) % NJ, (k + dk) % NK), device_id_type=MESH
-        )
-
-    def greet_plane(step, carry):
-        greet(step // NJ, step % NJ, 0)
-        return carry
-
-    def greet_sides(step, carry):
-        greet(step % NI, 0, 1)
-        greet(step % NI, 0, NK - 1)
-        return carry
-
-    def greet_lines(step, carry):
-        greet(0, step, 1)
-        greet(0, step, NK - 1)
-        return carry
-
-    lax.fori_loop(1, NI * NJ, greet_plane, 0)
-    lax.fori_loop(0, NI, greet_sides, 0)
-    lax.fori_loop(1, NJ, greet_lines, 0)
+    def greet(*device):
+        pl.semaphore_signal(barrier, inc=1, device_id=device, device_id_type=MESH)
+
+    for _, tk, there in sides:
+        @pl.when(there)
+        def _():
+            for ti in xs_of:
+                greet(ti, j, tk)
+            for tj in ys_of[1:]:
+                greet(i, tj, tk)
+
+    for ti in xs_of:
+        for tj in ys_of:
+            if ti is not i or tj is not j:
+                greet(ti, tj, k)
     at_end = (i == 0) | (i == NI - 1)
 
-    @pl.when(at_end)
-    def _():
-        dj = jnp.where(i == 0, NJ - 1, 1)
-
-        def greet_corners(step, carry):
-            greet(step, dj, 1)
-            greet(step, dj, NK - 1)
-            return carry
-
-        lax.fori_loop(0, NI, greet_corners, 0)
-
-    greeted = NI * NJ - 1 + 2 * NI + 2 * (NJ - 1) + 4
+    end_j = jnp.where(i == 0, ys_of[NJ - 1], ys_of[1])
+    for _, tk, there in sides:
+        @pl.when(there & at_end)
+        def _():
+            for ti in range(NI):
+                greet(ti, end_j, tk)
+
+    greeted = NI * NJ - 1 + side_count * (NI + NJ - 1 + 2)
 
     loads[0].wait()
     banded_weights(w_ref, wb)
@@ -144,6 +143,7 @@
     @pl.when(jnp.logical_not(at_end))
     def _():
         rows_in[...] = jnp.zeros_like(rows_in)
+        rims_y[...] = jnp.zeros_like(rims_y)
 
     loads[2].wait()
     pl.semaphore_wait(barrier, greeted)
@@ -159,26 +159,26 @@
             source, target, send, recv, device_id=device, device_id_type=MESH
         ).start()
 
-    def send_parts(step, carry):
-        to = (i + step) % NI
-        remote(part_rows(to), r1.at[i], r1_send, r1_recv, (to, j, k))
-        remote(pack.at[0], rims.at[i], t_send, t_recv, (to, j, (k + 1) % NK))
-        remote(pack.at[0], rims.at[NI + i], t_send, t_recv, (to, j, (k + NK - 1) % NK))
-        remote(mask_rows(to), mr.at[i], m_send, m_recv, (to, j, k))
-        return carry
-
-    for ti, dj, near in ((NI - 1, -1, 1), (0, 1, 3)):
-        tj = (j + dj) % NJ
-        remote(pack.at[near + 1], rows_in.at[NI + i], row_send, row_recv, (ti, tj, (k + 1) % NK))
-        remote(pack.at[near + 1], rows_in.at[2 * NI + i], row_send, row_recv, (ti, tj, (k + NK - 1) % NK))
+    ends = ((NI - 1, ys_of[NJ - 1], 1), (0, ys_of[1], 3))
+    for after, tk, there in sides:
+        @pl.when(there)
+        def _():
+            for ti, tj, near in ends:
+                remote(
+                    pack.at[near + 1], rims_y.at[1 - after, i], ry_send.at[after], ry_recv.at[1 - after],
+                    (ti, tj, tk),
+                )
+            for ti in xs_of:
+                remote(pack.at[0], rims.at[1 - after, i], t_send.at[after], t_recv.at[1 - after], (ti, j, tk))
+
+    for ti, tj, near in ends:
         remote(pack.at[near], rows_in.at[i], row_send, row_recv, (ti, tj, k))
-    lax.fori_loop(1, NI, send_parts, 0)
-    remote(pack.at[0], rims.at[i], t_send, t_recv, (i, j, (k + 1) % NK))
-    remote(pack.at[0], rims.at[NI + i], t_send, t_recv, (i, j, (k + NK - 1) % NK))
+    for ti in xs_of[1:]:
+        remote(mask_rows(ti), mr.at[i], m_send, m_recv, (ti, j, k))
+        remote(part_rows(ti), r1.at[i], r1_send, r1_recv, (ti, j, k))
     pltpu.make_async_copy(part_rows(i), r1.at[i], r1_recv).start()
     pltpu.make_async_copy(mask_rows(i), mr.at[i], m_recv).start()
 
-    first_z, last_z = k == 0, k == NK - 1
     outside = ((i == 0) & (j == 0)) | ((i == NI - 1) & (j == NJ - 1))
 
     def drain(ref, semaphore):
@@ -188,19 +188,27 @@
     def _():
         drain(rows_in, row_recv)
 
+    for after, tk, there in sides:
+        @pl.when(there & at_end)
+        def _():
+            drain(rims_y.at[after], ry_recv.at[after])
+
+        @pl.when(there)
+        def _():
+            drain(rims.at[after], t_recv.at[after])
+
     drain(r1, r1_recv)
-    drain(rims, t_recv)
     drain(mr, m_recv)
 
     end_row = sub == jnp.where(i == 0, 0, 7)
     parts = []
     for b in range(NI):
         both = jnp.where(
-            lane % 2 == 0, jnp.where(first_z, zero, rims[b]), jnp.where(last_z, zero, rims[NI + b])
+            lane % 2 == 0, jnp.where(first_z, zero, rims[0, b]), jnp.where(last_z, zero, rims[1, b])
         )
         both = pltpu.roll(both, (2 * BZ - 2 * i) % BZ, 1)
-        rows = rows_in[b] + jnp.where((lane == 0) & jnp.logical_not(first_z), rows_in[NI + b], 0.0)
-        rows += jnp.where((lane == BZ - 1) & jnp.logical_not(last_z), rows_in[2 * NI + b], 0.0)
+        rows = rows_in[b] + jnp.where((lane == 0) & jnp.logical_not(first_z), rims_y[0, b], 0.0)
+        rows += jnp.where((lane == BZ - 1) & jnp.logical_not(last_z), rims_y[1, b], 0.0)
         rows = jnp.where(outside, zero, rows)
         planes = []
         for p in range(PLANES):
@@ -237,26 +245,20 @@
             acc = jnp.concatenate([low, *middle, high], axis=0)
     xo[...] = acc
 
-    def send_x(step, carry):
-        peer = (i * NJ + j + step) % (NI * NJ)
-        remote(xo.at[peer], yb.at[j * NI + i], r2_send, r2_recv, (peer // NJ, peer % NJ, k))
-        return carry
-
-    lax.fori_loop(1, NI * NJ, send_x, 0)
+    for ti in xs_of:
+        for tj in ys_of:
+            if ti is not i or tj is not j:
+                remote(xo.at[ti * NJ + tj], yb.at[j * NI + i], r2_send, r2_recv, (ti, tj, k))
     pltpu.make_async_copy(xo.at[i * NJ + j], yb.at[j * NI + i], r2_recv).start()
 
-    def send_scores(step, carry):
-        to = (i + step) % NI
-        remote(sc.at[pl.ds(to * BX, BX)], scb.at[i], sc_send, sc_recv, (to, j, k))
-        return carry
-
-    lax.fori_loop(1, NI, send_scores, 0)
+    for ti in xs_of[1:]:
+        remote(sc.at[pl.ds(ti * BX, BX)], scb.at[i], sc_send, sc_recv, (ti, j, k))
     pltpu.make_async_copy(sc.at[pl.ds(i * BX, BX)], scb.at[i], sc_recv).start()
 
     drain(yb, r2_recv)
     yp[128:384] = yb[...].reshape(256, BZ)
 
-    for turn, to in enumerate(((j + 2) % NJ, NJ - 1 - j, j + 1 - 2 * (j % 2), j)):
+    for turn, to in enumerate((ys_of[2], NJ - 1 - j, NJ - 1 - ys_of[2], j)):
         base = pl.multiple_of(128 + to * BY, BY)
 
         def step_y(n, acc):
@@ -266,22 +268,32 @@
             return jnp.minimum(acc, jnp.minimum(low, high) + square)
 
         yo[turn] = lax.fori_loop(1, STEPS + 2, step_y, yp[pl.ds(base, BY), :], unroll=8)
-        for dk in (1, -1, 0):
-            if turn == 3 and dk == 0:
-                pltpu.make_async_copy(yo.at[turn], zb.at[NJ + j], r3_recv).start()
-            else:
+        for after, tk, there in sides:
+            @pl.when(there)
+            def _():
                 remote(
-                    yo.at[turn], zb.at[NJ * (1 - dk) + j], r3_send, r3_recv, (i, to, (k + dk) % NK)
+                    yo.at[turn], zb.at[2 * (1 - after), j], r3_send.at[2 * after], r3_recv.at[2 * (1 - after)],
+                    (i, to, tk),
                 )
+
+        if turn < NJ - 1:
+            remote(yo.at[turn], zb.at[1, j], r3_send.at[1], r3_recv.at[1], (i, to, k))
+        else:
+            pltpu.make_async_copy(yo.at[turn], zb.at[1, j], r3_recv.at[1]).start()
 
     drain(scb, sc_recv)
     for b in range(NI):
         score_ref[:, 8 * b : 8 * b + 8, :] = scb[b]
-    drain(zb, r3_recv)
+    drain(zb.at[1], r3_recv.at[1])
+    for after, tk, there in sides:
+        @pl.when(there)
+        def _():
+            drain(zb.at[2 * after], r3_recv.at[2 * after])
+
 
     for h in range(2):
         for d in range(3):
-            turned = zb[NJ * d + 2 * h : NJ * d + 2 * h + 2].reshape(128, BZ).T
+            turned = zb[d, 2 * h : 2 * h + 2].reshape(128, BZ).T
             if d == 0:
                 turned = jnp.where(first_z, FAR, turned)
             if d == 2:
@@ -301,10 +313,15 @@
     drain(mr.at[seven], m_send)
     drain(r1.at[seven], r1_send)
     drain(scb.at[seven], sc_send)
-    drain(rims, t_send)
-    drain(rows_in.at[pl.ds(0, 6)], row_send)
+    drain(rows_in.at[pl.ds(0, 2)], row_send)
     drain(yb.at[pl.ds(0, NI * NJ - 1)], r2_send)
-    drain(zb.at[pl.ds(0, 3 * NJ - 1)], r3_send)
+    drain(zb.at[1, pl.ds(0, NJ - 1)], r3_send.at[1])
+    for after, tk, there in sides:
+        @pl.when(there)
+        def _():
+            drain(rims_y.at[after, pl.ds(0, 2)], ry_send.at[after])
+            drain(rims.at[after], t_send.at[after])
+            drain(zb.at[2 * after], r3_send.at[2 * after])
 
 
 def shards(features, conv_weight, mask):
@@ -327,8 +344,9 @@
             pltpu.VMEM((PLANES, BY + 16, BZ), F32),
             pltpu.VMEM((5, *tile), F32),
             pltpu.VMEM((NI, PLANES, *tile), F32),
-            pltpu.VMEM((2 * NI, *tile), F32),
-            pltpu.VMEM((3 * NI, *tile), F32),
+            pltpu.VMEM((2, NI, *tile), F32),
+            pltpu.VMEM((2, NI, *tile), F32),
+            pltpu.VMEM((NI, *tile), F32),
             pltpu.VMEM((NI, BX, *tile), jnp.int32),
             pltpu.VMEM((32, *tile), F32),
             pltpu.VMEM((NI, BX, *tile), F32),
@@ -337,10 +355,10 @@
             pltpu.VMEM((32, *tile), F32),
             pltpu.VMEM((512, BZ), F32),
             pltpu.VMEM((NJ, BY, BZ), F32),
-            pltpu.VMEM((3 * NJ, BY, BZ), F32),
+            pltpu.VMEM((3, NJ, BY, BZ), F32),
             pltpu.VMEM((2, 384, BZ), F32),
             dma((3,)),
-        ] + [dma] * 14,
+        ] + [dma] * 10 + [dma((2,))] * 4 + [dma((3,))] * 2,
         compiler_params=pltpu.CompilerParams(
             collective_id=0, has_side_effects=True, vmem_limit_bytes=40 * 1024 * 1024
         ),

time: 41 us -> 37.7 us (0.920)
  the two profiles are of different devices: /device:TPU:1 before, /device:TPU:64 now
where the time goes in v2:
time: 37.7 us; the launch traced here: 37.6 us
  Pallas kernels  32.4 us (86%)
  local copies, waits for them, and re-layouts  4.5 us (12%)
  between operations  0.65 us (2%)
    pallas_call x1, Pallas kernels, shards(): pl.pallas_call(kernel, out_shape=(out, out), in_specs=[hbm] * 3, out_spec...  32.4 us
    unnamed x8, local copies, waits for them, and re-layouts  4.5 us

profile of v2, /device:TPU:64, one launch (start us, length us, event | category | flops | bytes accessed | tf_op | source)
XLA Modules:
  0.0 37.6 jit_solution(10820323610883180700)
XLA Ops:
  0.6 0.0 copy-start
  0.6 1.6 %copy-done = bf16[32,4,64,128]{3,2,1,0:T(8,128)(2,1)S(1)} copy-done((bf16[32,4,64,128]{3,2,1,0:T(8,128)(2,1)S(1)}, bf16[32,4,64,128]{3,2,1,0:T(8,128)(2,1)}, u32[]{:S(2)}) %copy-start) | copy-done | bytes 2097176
  2.2 0.0 copy-start.1
  2.2 0.9 %copy-done.1 = s32[4,64,128]{2,1,0:T(8,128)S(1)} copy-done((s32[4,64,128]{2,1,0:T(8,128)S(1)}, s32[4,64,128]{2,1,0:T(8,128)}, u32[]{:S(2)}) %copy-start.1) | copy-done | bytes 131096
  3.1 0.0 copy-start.2
  3.1 0.7 %copy-done.2 = bf16[27,32]{1,0:T(8,128)(2,1)S(1)} copy-done((bf16[27,32]{1,0:T(8,128)(2,1)S(1)}, bf16[27,32]{1,0:T(8,128)(2,1)}, u32[]{:S(2)}) %copy-start.2) | copy-done | bytes 1752
  3.8 32.4 %shard_map.50 = (f32[4,64,128]{2,1,0:T(8,128)S(1)}, f32[4,64,128]{2,1,0:T(8,128)S(1)}) custom-call(bf16[32,4,64,128]{3,2,1,0:T(8,128)(2,1)S(1)} %copy-done, bf16[27,32]{1,0:T(8,128)(2,1)S(1)} %copy-done.2, s32[4,64,128]{2,1,0:T(8,128)S(1)} %copy-done.1), custom_call_target="tpu_custom_call" | custom-call | tf_op jit(solution)/shard_map/pallas_call | solution.py:333
  36.3 0.7 %copy.7 = f32[4,64,128]{2,1,0:T(8,128)} copy(f32[4,64,128]{2,1,0:T(8,128)S(1)} %get-tuple-element.4) | data formatting | bytes 262144
  36.9 0.7 %copy.8 = f32[4,64,128]{2,1,0:T(8,128)} copy(f32[4,64,128]{2,1,0:T(8,128)S(1)} %get-tuple-element.5) | data formatting | bytes 262144
Async XLA Ops:
  0.6 1.6 %copy-start = (bf16[32,4,64,128]{3,2,1,0:T(8,128)(2,1)S(1)}, bf16[32,4,64,128]{3,2,1,0:T(8,128)(2,1)}, u32[]{:S(2)}) copy-start(bf16[32,4,64,128]{3,2,1,0:T(8,128)(2,1)} %f_hbm.1) | copy-start | bytes 6291460
  2.2 0.9 %copy-start.1 = (s32[4,64,128]{2,1,0:T(8,128)S(1)}, s32[4,64,128]{2,1,0:T(8,128)}, u32[]{:S(2)}) copy-start(s32[4,64,128]{2,1,0:T(8,128)} %m_hbm.1) | copy-start | bytes 393220
  3.1 0.7 %copy-start.2 = (bf16[27,32]{1,0:T(8,128)(2,1)S(1)}, bf16[27,32]{1,0:T(8,128)(2,1)}, u32[]{:S(2)}) copy-start(bf16[27,32]{1,0:T(8,128)(2,1)} %w_hbm.1) | copy-start | bytes 5188

commit v3 on v2

--- a/solution.py
+++ b/solution.py
@@ -41,9 +41,9 @@
 
 def kernel(
     f_hbm, w_hbm, m_hbm, score_ref, depth_ref,
-    f_ref, w_ref, m_ref, wb, s3, s, pack, r1, rims, rims_y, rows_in, mr, sc, scb, xin, xo, yb, yp, yo, zb, tz,
+    f_ref, w_ref, m_ref, wb, s3, s, pack, rim, r1, rims, rows_in, mr, sc, scb, xin, xo, yb, yp, yo, zb, tz,
     in_sems, m_send, m_recv, r1_send, r1_recv, row_send, row_recv, sc_send, sc_recv,
-    r2_send, r2_recv, t_send, t_recv, ry_send, ry_recv, r3_send, r3_recv,
+    r2_send, r2_recv, t_send, t_recv, r3_send, r3_recv,
 ):
     i, j, k = lax.axis_index("gx"), lax.axis_index("gy"), lax.axis_index("gz")
     loads = [
@@ -71,25 +71,13 @@
     for _, tk, there in sides:
         @pl.when(there)
         def _():
-            for ti in xs_of:
-                greet(ti, j, tk)
-            for tj in ys_of[1:]:
-                greet(i, tj, tk)
+            greet(i, j, tk)
 
     for ti in xs_of:
         for tj in ys_of:
             if ti is not i or tj is not j:
                 greet(ti, tj, k)
-    at_end = (i == 0) | (i == NI - 1)
-
-    end_j = jnp.where(i == 0, ys_of[NJ - 1], ys_of[1])
-    for _, tk, there in sides:
-        @pl.when(there & at_end)
-        def _():
-            for ti in range(NI):
-                greet(ti, end_j, tk)
-
-    greeted = NI * NJ - 1 + side_count * (NI + NJ - 1 + 2)
+    greeted = NI * NJ - 1 + side_count
 
     loads[0].wait()
     banded_weights(w_ref, wb)
@@ -122,20 +110,24 @@
             left = pltpu.roll(s3[2, p, rows, :], BZ - 1, 1)
             mine = s3[1, p, rows, :] + jnp.where(lane == 0, 0.0, right) + jnp.where(lane == BZ - 1, 0.0, left)
             s[p, rows, :] = mine
-            rim = jnp.where(lane == 0, right, left)
+            outer = jnp.where(lane == 0, right, left)
             if t == 0:
                 pack[1, pl.ds(p, 1), :] = mine[7:8]
-                pack[2, pl.ds(p, 1), :] = rim[7:8]
+                pack[2, pl.ds(p, 1), :] = outer[7:8]
             elif t == 9:
                 pack[3, pl.ds(p, 1), :] = mine[0:1]
-                pack[4, pl.ds(p, 1), :] = rim[0:1]
+                pack[4, pl.ds(p, 1), :] = outer[0:1]
             else:
                 v = 2 * (p * 8 + t - 1)
-                moved = pltpu.roll(rim, v, 1)
+                moved = pltpu.roll(outer, v, 1)
                 tile = jnp.where((lane == v) | (lane == (v + BZ - 1) % BZ), moved, tile)
         return tile
 
-    pack[0] = lax.fori_loop(0, PLANES, shift_plane, zero)
+    tile = lax.fori_loop(0, PLANES, shift_plane, zero)
+    for near, v in ((2, 96), (4, 98)):
+        tile = jnp.where((lane == v) | (lane == v - 1), pltpu.roll(pack[near], v, 1), tile)
+    rim[...] = tile
+    at_end = (i == 0) | (i == NI - 1)
     far = jnp.full((128, BZ), FAR, F32)
     yp[0:128] = far
     yp[384:512] = far
@@ -143,79 +135,74 @@
     @pl.when(jnp.logical_not(at_end))
     def _():
         rows_in[...] = jnp.zeros_like(rows_in)
-        rims_y[...] = jnp.zeros_like(rims_y)
 
     loads[2].wait()
     pl.semaphore_wait(barrier, greeted)
-
-    def part_rows(to):
-        return s.at[:, pl.ds(pl.multiple_of(8 + to * 8, 8), 8), :]
-
-    def mask_rows(to):
-        return m_ref.at[:, pl.ds(pl.multiple_of(to * 8, 8), 8), :]
 
     def remote(source, target, send, recv, device):
         pltpu.make_async_remote_copy(
             source, target, send, recv, device_id=device, device_id_type=MESH
         ).start()
 
-    ends = ((NI - 1, ys_of[NJ - 1], 1), (0, ys_of[1], 3))
+    def drain(ref, semaphore):
+        pltpu.make_async_copy(ref, ref, semaphore).wait()
+
     for after, tk, there in sides:
         @pl.when(there)
         def _():
-            for ti, tj, near in ends:
-                remote(
-                    pack.at[near + 1], rims_y.at[1 - after, i], ry_send.at[after], ry_recv.at[1 - after],
-                    (ti, tj, tk),
-                )
-            for ti in xs_of:
-                remote(pack.at[0], rims.at[1 - after, i], t_send.at[after], t_recv.at[1 - after], (ti, j, tk))
-
-    for ti, tj, near in ends:
-        remote(pack.at[near], rows_in.at[i], row_send, row_recv, (ti, tj, k))
+            remote(rim, rims.at[1 - after], t_send.at[after], t_recv.at[1 - after], (i, j, tk))
+
+    def mask_rows(to):
+        return m_ref.at[:, pl.ds(pl.multiple_of(to * 8, 8), 8), :]
+
     for ti in xs_of[1:]:
         remote(mask_rows(ti), mr.at[i], m_send, m_recv, (ti, j, k))
+    pltpu.make_async_copy(mask_rows(i), mr.at[i], m_recv).start()
+
+    for after, tk, there in sides:
+        @pl.when(there)
+        def _():
+            drain(rims.at[after], t_recv.at[after])
+
+    both = jnp.where(lane % 2 == 0, jnp.where(first_z, zero, rims[0]), jnp.where(last_z, zero, rims[1]))
+    for near, v in ((1, 96), (3, 98)):
+        pack[near] += jnp.where(edge, pltpu.roll(both, BZ - v, 1), 0.0)
+
+    def add_rims(p, turned):
+        for t in range(8):
+            rows = pl.ds(8 * t + 8, 8)
+            moved = turned if t == 0 else pltpu.roll(turned, BZ - 2 * t, 1)
+            s[p, rows, :] += jnp.where(edge, moved, 0.0)
+        return pltpu.roll(turned, BZ - 16, 1)
+
+    lax.fori_loop(0, PLANES, add_rims, both)
+
+    def part_rows(to):
+        return s.at[:, pl.ds(pl.multiple_of(8 + to * 8, 8), 8), :]
+
+    for ti in xs_of[1:]:
         remote(part_rows(ti), r1.at[i], r1_send, r1_recv, (ti, j, k))
+    for ti, tj, near in ((NI - 1, ys_of[NJ - 1], 1), (0, ys_of[1], 3)):
+        remote(pack.at[near], rows_in.at[i], row_send, row_recv, (ti, tj, k))
     pltpu.make_async_copy(part_rows(i), r1.at[i], r1_recv).start()
-    pltpu.make_async_copy(mask_rows(i), mr.at[i], m_recv).start()
-
     outside = ((i == 0) & (j == 0)) | ((i == NI - 1) & (j == NJ - 1))
-
-    def drain(ref, semaphore):
-        pltpu.make_async_copy(ref, ref, semaphore).wait()
 
     @pl.when(at_end)
     def _():
         drain(rows_in, row_recv)
 
-    for after, tk, there in sides:
-        @pl.when(there & at_end)
-        def _():
-            drain(rims_y.at[after], ry_recv.at[after])
-
-        @pl.when(there)
-        def _():
-            drain(rims.at[after], t_recv.at[after])
-
     drain(r1, r1_recv)
     drain(mr, m_recv)
 
     end_row = sub == jnp.where(i == 0, 0, 7)
     parts = []
     for b in range(NI):
-        both = jnp.where(
-            lane % 2 == 0, jnp.where(first_z, zero, rims[0, b]), jnp.where(last_z, zero, rims[1, b])
-        )
-        both = pltpu.roll(both, (2 * BZ - 2 * i) % BZ, 1)
-        rows = rows_in[b] + jnp.where((lane == 0) & jnp.logical_not(first_z), rims_y[0, b], 0.0)
-        rows += jnp.where((lane == BZ - 1) & jnp.logical_not(last_z), rims_y[1, b], 0.0)
+        rows = rows_in[b]
         rows = jnp.where(outside, zero, rows)
         planes = []
         for p in range(PLANES):
-            moved = both if p == 0 else pltpu.roll(both, BZ - 16 * p, 1)
             planes.append(
                 r1[b, p]
-                + jnp.where(edge, moved, 0.0)
                 + jnp.where(end_row, jnp.broadcast_to(rows[p : p + 1], (8, BZ)), 0.0)
             )
         parts.append(planes)
@@ -260,6 +247,7 @@
 
     for turn, to in enumerate((ys_of[2], NJ - 1 - j, NJ - 1 - ys_of[2], j)):
         base = pl.multiple_of(128 + to * BY, BY)
+        far_chip = 1 if turn < 2 else 0
 
         def step_y(n, acc):
             square = (n * n).astype(F32)
@@ -272,28 +260,30 @@
             @pl.when(there)
             def _():
                 remote(
-                    yo.at[turn], zb.at[2 * (1 - after), j], r3_send.at[2 * after], r3_recv.at[2 * (1 - after)],
+                    yo.at[turn], zb.at[2 * (1 - after), j], r3_send.at[2 * after],
+                    r3_recv.at[2 * (1 - after), far_chip],
                     (i, to, tk),
                 )
 
         if turn < NJ - 1:
-            remote(yo.at[turn], zb.at[1, j], r3_send.at[1], r3_recv.at[1], (i, to, k))
+            remote(yo.at[turn], zb.at[1, j], r3_send.at[1], r3_recv.at[1, far_chip], (i, to, k))
         else:
-            pltpu.make_async_copy(yo.at[turn], zb.at[1, j], r3_recv.at[1]).start()
+            pltpu.make_async_copy(yo.at[turn], zb.at[1, j], r3_recv.at[1, far_chip]).start()
 
     drain(scb, sc_recv)
     for b in range(NI):
         score_ref[:, 8 * b : 8 * b + 8, :] = scb[b]
-    drain(zb.at[1], r3_recv.at[1])
-    for after, tk, there in sides:
-        @pl.when(there)
-        def _():
-            drain(zb.at[2 * after], r3_recv.at[2 * after])
-
-
-    for h in range(2):
+    own_pair = jnp.where(j >= 2, 2, 0)
+    for h, pair in enumerate((own_pair, 2 - own_pair)):
+        two = pl.ds(pair, 2)
+        drain(zb.at[1, two], r3_recv.at[1, h])
+        for after, tk, there in sides:
+            @pl.when(there)
+            def _():
+                drain(zb.at[2 * after, two], r3_recv.at[2 * after, h])
+
         for d in range(3):
-            turned = zb[d, 2 * h : 2 * h + 2].reshape(128, BZ).T
+            turned = zb[d, two].reshape(128, BZ).T
             if d == 0:
                 turned = jnp.where(first_z, FAR, turned)
             if d == 2:
@@ -307,7 +297,7 @@
             return jnp.minimum(acc, jnp.minimum(low, high) + square)
 
         least = lax.fori_loop(1, STEPS + 2, step_z, tz[h, 128:256, :], unroll=4)
-        depth_ref[2 * h : 2 * h + 2] = (least * (1.0 / RADIUS)).T.reshape(2, BY, BZ)
+        depth_ref[two] = (least * (1.0 / RADIUS)).T.reshape(2, BY, BZ)
 
     seven = pl.ds(0, NI - 1)
     drain(mr.at[seven], m_send)
@@ -319,7 +309,6 @@
     for after, tk, there in sides:
         @pl.when(there)
         def _():
-            drain(rims_y.at[after, pl.ds(0, 2)], ry_send.at[after])
             drain(rims.at[after], t_send.at[after])
             drain(zb.at[2 * after], r3_send.at[2 * after])
 
@@ -343,9 +332,9 @@
             pltpu.VMEM((3, PLANES, BY + 16, BZ), F32),
             pltpu.VMEM((PLANES, BY + 16, BZ), F32),
             pltpu.VMEM((5, *tile), F32),
+            pltpu.VMEM(tile, F32),
             pltpu.VMEM((NI, PLANES, *tile), F32),
-            pltpu.VMEM((2, NI, *tile), F32),
-            pltpu.VMEM((2, NI, *tile), F32),
+            pltpu.VMEM((2, *tile), F32),
             pltpu.VMEM((NI, *tile), F32),
             pltpu.VMEM((NI, BX, *tile), jnp.int32),
             pltpu.VMEM((32, *tile), F32),
@@ -358,7 +347,7 @@
             pltpu.VMEM((3, NJ, BY, BZ), F32),
             pltpu.VMEM((2, 384, BZ), F32),
             dma((3,)),
-        ] + [dma] * 10 + [dma((2,))] * 4 + [dma((3,))] * 2,
+        ] + [dma] * 10 + [dma((2,))] * 2 + [dma((3,)), dma((3, 2))],
         compiler_params=pltpu.CompilerParams(
             collective_id=0, has_side_effects=True, vmem_limit_bytes=40 * 1024 * 1024
         ),

time: 37.7 us -> 37.5 us (level)
  no operation moved by 1% of the time
where the time goes in v3:
time: 37.5 us; the launch traced here: 37.3 us
  Pallas kernels  32.2 us (86%)
  local copies, waits for them, and re-layouts  4.5 us (12%)
  between operations  0.65 us (2%)
    pallas_call x1, Pallas kernels, shards(): pl.pallas_call(kernel, out_shape=(out, out), in_specs=[hbm] * 3, out_spec...  32.2 us
    unnamed x8, local copies, waits for them, and re-layouts  4.5 us

profile of v3, /device:TPU:64, one launch (start us, length us, event | category | flops | bytes accessed | tf_op | source)
XLA Modules:
  0.0 37.3 jit_solution(9512489056999821371)
XLA Ops:
  0.6 0.0 copy-start
  0.6 1.6 %copy-done = bf16[32,4,64,128]{3,2,1,0:T(8,128)(2,1)S(1)} copy-done((bf16[32,4,64,128]{3,2,1,0:T(8,128)(2,1)S(1)}, bf16[32,4,64,128]{3,2,1,0:T(8,128)(2,1)}, u32[]{:S(2)}) %copy-start) | copy-done | bytes 2097176
  2.2 0.0 copy-start.1
  2.2 0.9 %copy-done.1 = s32[4,64,128]{2,1,0:T(8,128)S(1)} copy-done((s32[4,64,128]{2,1,0:T(8,128)S(1)}, s32[4,64,128]{2,1,0:T(8,128)}, u32[]{:S(2)}) %copy-start.1) | copy-done | bytes 131096
  3.1 0.0 copy-start.2
  3.1 0.7 %copy-done.2 = bf16[27,32]{1,0:T(8,128)(2,1)S(1)} copy-done((bf16[27,32]{1,0:T(8,128)(2,1)S(1)}, bf16[27,32]{1,0:T(8,128)(2,1)}, u32[]{:S(2)}) %copy-start.2) | copy-done | bytes 1752
  3.8 32.2 %shard_map.50 = (f32[4,64,128]{2,1,0:T(8,128)S(1)}, f32[4,64,128]{2,1,0:T(8,128)S(1)}) custom-call(bf16[32,4,64,128]{3,2,1,0:T(8,128)(2,1)S(1)} %copy-done, bf16[27,32]{1,0:T(8,128)(2,1)S(1)} %copy-done.2, s32[4,64,128]{2,1,0:T(8,128)S(1)} %copy-done.1), custom_call_target="tpu_custom_call" | custom-call | tf_op jit(solution)/shard_map/pallas_call | solution.py:322
  36.0 0.7 %copy.7 = f32[4,64,128]{2,1,0:T(8,128)} copy(f32[4,64,128]{2,1,0:T(8,128)S(1)} %get-tuple-element.4) | data formatting | bytes 262144
  36.7 0.7 %copy.8 = f32[4,64,128]{2,1,0:T(8,128)} copy(f32[4,64,128]{2,1,0:T(8,128)S(1)} %get-tuple-element.5) | data formatting | bytes 262144
Async XLA Ops:
  0.6 1.6 %copy-start = (bf16[32,4,64,128]{3,2,1,0:T(8,128)(2,1)S(1)}, bf16[32,4,64,128]{3,2,1,0:T(8,128)(2,1)}, u32[]{:S(2)}) copy-start(bf16[32,4,64,128]{3,2,1,0:T(8,128)(2,1)} %f_hbm.1) | copy-start | bytes 6291460
  2.2 0.9 %copy-start.1 = (s32[4,64,128]{2,1,0:T(8,128)S(1)}, s32[4,64,128]{2,1,0:T(8,128)}, u32[]{:S(2)}) copy-start(s32[4,64,128]{2,1,0:T(8,128)} %m_hbm.1) | copy-start | bytes 393220
  3.1 0.7 %copy-start.2 = (bf16[27,32]{1,0:T(8,128)(2,1)S(1)}, bf16[27,32]{1,0:T(8,128)(2,1)}, u32[]{:S(2)}) copy-start(bf16[27,32]{1,0:T(8,128)(2,1)} %w_hbm.1) | copy-start | bytes 5188

commit v4 on v3

--- a/solution.py
+++ b/solution.py
@@ -40,7 +40,7 @@
 
 
 def kernel(
-    f_hbm, w_hbm, m_hbm, score_ref, depth_ref,
+    f_hbm, w_hbm, m_hbm, score_ref, least_ref,
     f_ref, w_ref, m_ref, wb, s3, s, pack, rim, r1, rims, rows_in, mr, sc, scb, xin, xo, yb, yp, yo, zb, tz,
     in_sems, m_send, m_recv, r1_send, r1_recv, row_send, row_recv, sc_send, sc_recv,
     r2_send, r2_recv, t_send, t_recv, r3_send, r3_recv,
@@ -296,8 +296,8 @@
             high = tz[h, pl.ds(128 + n, 128), :]
             return jnp.minimum(acc, jnp.minimum(low, high) + square)
 
-        least = lax.fori_loop(1, STEPS + 2, step_z, tz[h, 128:256, :], unroll=4)
-        depth_ref[two] = (least * (1.0 / RADIUS)).T.reshape(2, BY, BZ)
+        first = jnp.where(pair == 0, 0, 1)
+        least_ref[first] = lax.fori_loop(1, STEPS + 2, step_z, tz[h, 128:256, :], unroll=4)
 
     seven = pl.ds(0, NI - 1)
     drain(mr.at[seven], m_send)
@@ -313,15 +313,27 @@
             drain(zb.at[2 * after], r3_send.at[2 * after])
 
 
+def finish(score_in, least_ref, score_hbm, depth_hbm, depth, sems):
+    copies = [pltpu.make_async_copy(score_in, score_hbm, sems.at[2])]
+    copies[0].start()
+    for h in range(2):
+        planes = pl.ds(2 * h, 2)
+        depth[planes] = (least_ref[h] * (1.0 / RADIUS)).T.reshape(2, BY, BZ)
+        copies.append(pltpu.make_async_copy(depth.at[planes], depth_hbm.at[planes], sems.at[h]))
+        copies[-1].start()
+    for copy in copies:
+        copy.wait()
+
+
 def shards(features, conv_weight, mask):
     vmem = pl.BlockSpec(memory_space=pltpu.VMEM)
     hbm = pl.BlockSpec(memory_space=pltpu.HBM)
     tile = (8, BZ)
     dma = pltpu.SemaphoreType.DMA
     out = jax.ShapeDtypeStruct((BX, BY, BZ), F32)
-    return pl.pallas_call(
+    score, least = pl.pallas_call(
         kernel,
-        out_shape=(out, out),
+        out_shape=(out, jax.ShapeDtypeStruct((2, 128, BZ), F32)),
         in_specs=[hbm] * 3,
         out_specs=(vmem, vmem),
         scratch_shapes=[
@@ -351,7 +363,15 @@
         compiler_params=pltpu.CompilerParams(
             collective_id=0, has_side_effects=True, vmem_limit_bytes=40 * 1024 * 1024
         ),
-    )(features, conv_weight, mask)
+    )(*[pltpu.with_memory_space_constraint(x, pltpu.HBM) for x in (features, conv_weight, mask)])
+    return pl.pallas_call(
+        finish,
+        out_shape=(out, out),
+        in_specs=[vmem] * 2,
+        out_specs=(hbm, hbm),
+        scratch_shapes=[pltpu.VMEM((BX, BY, BZ), F32), dma((3,))],
+        compiler_params=pltpu.CompilerParams(vmem_limit_bytes=2 * 1024 * 1024),
+    )(score, least)
 
 
 def solution(mesh):

time: 37.5 us -> 33.6 us (0.90)
  local copies, waits for them, and re-layouts: 4.5 us -> 0 us
  Pallas kernels: 32.2 us -> 32.8 us
    unnamed x8 -> x0, local copies, waits for them, and re-layouts: 4.5 us -> none
    pallas_call x1 -> x2, Pallas kernels: 32.2 us -> 32.8 us  [the longest x1 32 us: shards(): pl.pallas_call(kernel, out_shape=(out, jax.ShapeDtypeStruct((2, 128, BZ),...]
where the time goes in v4:
time: 33.6 us; the launch traced here: 33.4 us
  Pallas kernels  32.8 us (98%)
  between operations  0.64 us (2%)
    pallas_call x1, Pallas kernels, shards(): pl.pallas_call(kernel, out_shape=(out, jax.ShapeDtypeStruct((2, 128, BZ),...  32 us
    pallas_call x1, Pallas kernels, shards(): pl.pallas_call(finish, out_shape=(out, out), in_specs=[vmem] * 2, out_spe...  0.78 us

profile of v4, /device:TPU:64, one launch (start us, length us, event | category | flops | bytes accessed | tf_op | source)
XLA Modules:
  0.0 33.4 jit_solution(5883613027902498494)
XLA Ops:
  0.6 32.0 %shard_map.50 = (f32[4,64,128]{2,1,0:T(8,128)S(1)}, f32[2,128,128]{2,1,0:T(8,128)S(1)}) custom-call(bf16[32,4,64,128]{3,2,1,0:T(8,128)(2,1)} %f_hbm.1, bf16[27,32]{1,0:T(8,128)(2,1)} %w_hbm.1, s32[4,64,128]{2,1,0:T(8,128)} %m_hbm.1), custom_call_target="tpu_custom_call" | custom-call | tf_op jit(solution)/shard_map/pallas_call | solution.py:334
  32.7 0.8 %shard_map.51 = (f32[4,64,128]{2,1,0:T(8,128)}, f32[4,64,128]{2,1,0:T(8,128)}) custom-call(f32[4,64,128]{2,1,0:T(8,128)S(1)} %get-tuple-element.4.score_in, f32[2,128,128]{2,1,0:T(8,128)S(1)} %get-tuple-element.5.least_ref), custom_call_target="tpu_custom_call" | custom-call | tf_op jit(solution)/shard_map/pallas_call | solution.py:367

commit v5 on v4

--- a/solution.py
+++ b/solution.py
@@ -59,6 +59,8 @@
         ]
 
     xs_of, ys_of = around(i, NI), around(j, NJ)
+    xs_of = [xs_of[d] for d in (0, 3, 5, 4, 1, 7, 2, 6)]
+    ys_far = [ys_of[d] for d in (2, 3, 1, 0)]
     first_z, last_z = k == 0, k == NK - 1
     sides = ((1, k + 1, jnp.logical_not(last_z)), (0, k - 1, jnp.logical_not(first_z)))
     side_count = 2 - first_z.astype(jnp.int32) - last_z.astype(jnp.int32)
@@ -73,8 +75,8 @@
         def _():
             greet(i, j, tk)
 
-    for ti in xs_of:
-        for tj in ys_of:
+    for ti in xs_of[1:] + [i]:
+        for tj in ys_far:
             if ti is not i or tj is not j:
                 greet(ti, tj, k)
     greeted = NI * NJ - 1 + side_count
@@ -131,6 +133,9 @@
     far = jnp.full((128, BZ), FAR, F32)
     yp[0:128] = far
     yp[384:512] = far
+    for h in range(2):
+        tz[h, 0:128] = far
+        tz[h, 256:384] = far
 
     @pl.when(jnp.logical_not(at_end))
     def _():
@@ -232,8 +237,8 @@
             acc = jnp.concatenate([low, *middle, high], axis=0)
     xo[...] = acc
 
-    for ti in xs_of:
-        for tj in ys_of:
+    for ti in xs_of[1:] + [i]:
+        for tj in ys_far:
             if ti is not i or tj is not j:
                 remote(xo.at[ti * NJ + tj], yb.at[j * NI + i], r2_send, r2_recv, (ti, tj, k))
     pltpu.make_async_copy(xo.at[i * NJ + j], yb.at[j * NI + i], r2_recv).start()
@@ -274,30 +279,56 @@
     for b in range(NI):
         score_ref[:, 8 * b : 8 * b + 8, :] = scb[b]
     own_pair = jnp.where(j >= 2, 2, 0)
-    for h, pair in enumerate((own_pair, 2 - own_pair)):
+    pairs = tuple(enumerate((own_pair, 2 - own_pair)))
+
+    for h, pair in pairs:
+        drain(zb.at[1, pl.ds(pair, 2)], r3_recv.at[1, h])
+        tz[h, 128:256, :] = zb[1, pl.ds(pair, 2)].reshape(128, BZ).T
+
+        def near_z(n, acc):
+            square = (n * n).astype(F32)
+            low = tz[h, pl.ds(128 - n, 128), :]
+            high = tz[h, pl.ds(128 + n, 128), :]
+            return jnp.minimum(acc, jnp.minimum(low, high) + square)
+
+        def far_z(n, halves):
+            square = (n * n).astype(F32)
+            low, high = halves
+            low = jnp.minimum(low, tz[h, pl.ds(128 + n, 64), :] + square)
+            high = jnp.minimum(high, tz[h, pl.ds(192 - n, 64), :] + square)
+            return low, high
+
+        acc = lax.fori_loop(1, 65, near_z, tz[h, 128:256, :], unroll=4)
+        low, high = lax.fori_loop(65, 129, far_z, (acc[0:64], acc[64:128]), unroll=4)
+        first = pair // 2
+        least_ref[first, 0:64, :] = low
+        least_ref[first, 64:128, :] = high
+
+    for h, pair in pairs:
         two = pl.ds(pair, 2)
-        drain(zb.at[1, two], r3_recv.at[1, h])
         for after, tk, there in sides:
             @pl.when(there)
             def _():
                 drain(zb.at[2 * after, two], r3_recv.at[2 * after, h])
 
-        for d in range(3):
-            turned = zb[d, two].reshape(128, BZ).T
-            if d == 0:
-                turned = jnp.where(first_z, FAR, turned)
-            if d == 2:
-                turned = jnp.where(last_z, FAR, turned)
-            tz[h, 128 * d : 128 * d + 128, :] = turned
-
-        def step_z(n, acc):
-            square = (n * n).astype(F32)
-            low = tz[h, pl.ds(128 - n, 128), :]
-            high = tz[h, pl.ds(128 + n, 128), :]
-            return jnp.minimum(acc, jnp.minimum(low, high) + square)
-
-        first = jnp.where(pair == 0, 0, 1)
-        least_ref[first] = lax.fori_loop(1, STEPS + 2, step_z, tz[h, 128:256, :], unroll=4)
+        before = zb[0, two].reshape(128, BZ).T
+        tz[h, 0:128, :] = jnp.where(first_z, FAR, before)
+        later = zb[2, two].reshape(128, BZ).T
+        tz[h, 256:384, :] = jnp.where(last_z, FAR, later)
+        first = pair // 2
+        for block in range(16):
+            size = 8 * block + 8
+
+            def from_before(n, acc):
+                return jnp.minimum(acc, tz[h, pl.ds(128 - n, size), :] + (n * n).astype(F32))
+
+            def from_later(n, acc):
+                return jnp.minimum(acc, tz[h, pl.ds(256 - size + n, size), :] + (n * n).astype(F32))
+
+            span = (size - 7, size + 1)
+            least_ref[first, 0:size, :] = lax.fori_loop(*span, from_before, least_ref[first, 0:size, :], unroll=8)
+            rest = slice(128 - size, 128)
+            least_ref[first, rest, :] = lax.fori_loop(*span, from_later, least_ref[first, rest, :], unroll=8)
 
     seven = pl.ds(0, NI - 1)
     drain(mr.at[seven], m_send)

time: 33.6 us -> 31.7 us (0.943); the launches traced: 33.4 us -> 31.2 us
  Pallas kernels: 32.8 us -> 30.5 us
    pallas_call x1, Pallas kernels: 32 us -> 29.7 us  [shards(): pl.pallas_call(kernel, out_shape=(out, jax.ShapeDtypeStruct((2, 128, BZ),...]
where the time goes in v5:
time: 31.7 us; the launch traced here: 31.2 us
  Pallas kernels  30.5 us (96%)
  between operations  0.64 us (2%)
    pallas_call x1, Pallas kernels, shards(): pl.pallas_call(kernel, out_shape=(out, jax.ShapeDtypeStruct((2, 128, BZ),...  29.7 us
    pallas_call x1, Pallas kernels, shards(): pl.pallas_call(finish, out_shape=(out, out), in_specs=[vmem] * 2, out_spe...  0.78 us

profile of v5, /device:TPU:64, one launch (start us, length us, event | category | flops | bytes accessed | tf_op | source)
XLA Modules:
  0.0 31.2 jit_solution(15463281038780905636)
XLA Ops:
  0.6 29.7 %shard_map.50 = (f32[4,64,128]{2,1,0:T(8,128)S(1)}, f32[2,128,128]{2,1,0:T(8,128)S(1)}) custom-call(bf16[32,4,64,128]{3,2,1,0:T(8,128)(2,1)} %f_hbm.1, bf16[27,32]{1,0:T(8,128)(2,1)} %w_hbm.1, s32[4,64,128]{2,1,0:T(8,128)} %m_hbm.1), custom_call_target="tpu_custom_call" | custom-call | tf_op jit(solution)/shard_map/pallas_call | solution.py:365
  30.4 0.8 %shard_map.51 = (f32[4,64,128]{2,1,0:T(8,128)}, f32[4,64,128]{2,1,0:T(8,128)}) custom-call(f32[4,64,128]{2,1,0:T(8,128)S(1)} %get-tuple-element.4.score_in, f32[2,128,128]{2,1,0:T(8,128)S(1)} %get-tuple-element.5.least_ref), custom_call_target="tpu_custom_call" | custom-call | tf_op jit(solution)/shard_map/pallas_call | solution.py:398

commit v6 on v5

--- a/solution.py
+++ b/solution.py
@@ -41,9 +41,9 @@
 
 def kernel(
     f_hbm, w_hbm, m_hbm, score_ref, least_ref,
-    f_ref, w_ref, m_ref, wb, s3, s, pack, rim, r1, rims, rows_in, mr, sc, scb, xin, xo, yb, yp, yo, zb, tz,
+    f_ref, w_ref, m_ref, wb, s3, s, pack, rim, r1, rims, rims_y, rows_in, mb, mr, sc, scb, xin, xo, yb, yp, yo, zb, tz,
     in_sems, m_send, m_recv, r1_send, r1_recv, row_send, row_recv, sc_send, sc_recv,
-    r2_send, r2_recv, t_send, t_recv, r3_send, r3_recv,
+    r2_send, r2_recv, t_send, t_recv, ry_send, ry_recv, r3_send, r3_recv,
 ):
     i, j, k = lax.axis_index("gx"), lax.axis_index("gy"), lax.axis_index("gz")
     loads = [
@@ -73,13 +73,22 @@
     for _, tk, there in sides:
         @pl.when(there)
         def _():
-            greet(i, j, tk)
+            for ti in xs_of:
+                greet(ti, j, tk)
 
     for ti in xs_of[1:] + [i]:
         for tj in ys_far:
             if ti is not i or tj is not j:
                 greet(ti, tj, k)
-    greeted = NI * NJ - 1 + side_count
+    at_end = (i == 0) | (i == NI - 1)
+    end_j = jnp.where(i == 0, ys_of[NJ - 1], ys_of[1])
+    for _, tk, there in sides:
+        @pl.when(there & at_end)
+        def _():
+            for ti in range(NI):
+                greet(ti, end_j, tk)
+
+    greeted = NI * NJ - 1 + side_count * (NI + 2)
 
     loads[0].wait()
     banded_weights(w_ref, wb)
@@ -129,7 +138,6 @@
     for near, v in ((2, 96), (4, 98)):
         tile = jnp.where((lane == v) | (lane == v - 1), pltpu.roll(pack[near], v, 1), tile)
     rim[...] = tile
-    at_end = (i == 0) | (i == NI - 1)
     far = jnp.full((128, BZ), FAR, F32)
     yp[0:128] = far
     yp[384:512] = far
@@ -140,8 +148,11 @@
     @pl.when(jnp.logical_not(at_end))
     def _():
         rows_in[...] = jnp.zeros_like(rows_in)
+        rims_y[...] = jnp.zeros_like(rims_y)
 
     loads[2].wait()
+    for b in range(NI):
+        mb[b] = m_ref[:, 8 * b : 8 * b + 8, :].reshape(32, BZ).astype(F32).astype(jnp.bfloat16)
     pl.semaphore_wait(barrier, greeted)
 
     def remote(source, target, send, recv, device):
@@ -152,66 +163,74 @@
     def drain(ref, semaphore):
         pltpu.make_async_copy(ref, ref, semaphore).wait()
 
+    ends = ((NI - 1, ys_of[NJ - 1], 1), (0, ys_of[1], 3))
     for after, tk, there in sides:
         @pl.when(there)
         def _():
-            remote(rim, rims.at[1 - after], t_send.at[after], t_recv.at[1 - after], (i, j, tk))
-
+            for ti in xs_of[1:] + [i]:
+                remote(rim, rims.at[1 - after, i], t_send.at[after], t_recv.at[1 - after], (ti, j, tk))
+            for ti, tj, near in ends:
+                remote(
+                    rim, rims_y.at[1 - after, i], ry_send.at[after], ry_recv.at[1 - after], (ti, tj, tk)
+                )
+
+    def part_rows(to):
+        return s.at[:, pl.ds(pl.multiple_of(8 + to * 8, 8), 8), :]
+
+    for ti in xs_of[1:]:
+        remote(part_rows(ti), r1.at[i], r1_send, r1_recv, (ti, j, k))
+    for ti, tj, near in ends:
+        remote(pack.at[near], rows_in.at[i], row_send, row_recv, (ti, tj, k))
+    pltpu.make_async_copy(part_rows(i), r1.at[i], r1_recv).start()
     def mask_rows(to):
-        return m_ref.at[:, pl.ds(pl.multiple_of(to * 8, 8), 8), :]
+        return mb.at[to]
 
     for ti in xs_of[1:]:
         remote(mask_rows(ti), mr.at[i], m_send, m_recv, (ti, j, k))
     pltpu.make_async_copy(mask_rows(i), mr.at[i], m_recv).start()
 
-    for after, tk, there in sides:
-        @pl.when(there)
-        def _():
-            drain(rims.at[after], t_recv.at[after])
-
-    both = jnp.where(lane % 2 == 0, jnp.where(first_z, zero, rims[0]), jnp.where(last_z, zero, rims[1]))
-    for near, v in ((1, 96), (3, 98)):
-        pack[near] += jnp.where(edge, pltpu.roll(both, BZ - v, 1), 0.0)
-
-    def add_rims(p, turned):
-        for t in range(8):
-            rows = pl.ds(8 * t + 8, 8)
-            moved = turned if t == 0 else pltpu.roll(turned, BZ - 2 * t, 1)
-            s[p, rows, :] += jnp.where(edge, moved, 0.0)
-        return pltpu.roll(turned, BZ - 16, 1)
-
-    lax.fori_loop(0, PLANES, add_rims, both)
-
-    def part_rows(to):
-        return s.at[:, pl.ds(pl.multiple_of(8 + to * 8, 8), 8), :]
-
-    for ti in xs_of[1:]:
-        remote(part_rows(ti), r1.at[i], r1_send, r1_recv, (ti, j, k))
-    for ti, tj, near in ((NI - 1, ys_of[NJ - 1], 1), (0, ys_of[1], 3)):
-        remote(pack.at[near], rows_in.at[i], row_send, row_recv, (ti, tj, k))
-    pltpu.make_async_copy(part_rows(i), r1.at[i], r1_recv).start()
     outside = ((i == 0) & (j == 0)) | ((i == NI - 1) & (j == NJ - 1))
 
     @pl.when(at_end)
     def _():
         drain(rows_in, row_recv)
 
+    for after, tk, there in sides:
+        @pl.when(there & at_end)
+        def _():
+            drain(rims_y.at[after], ry_recv.at[after])
+
+        @pl.when(there)
+        def _():
+            drain(rims.at[after], t_recv.at[after])
+
     drain(r1, r1_recv)
     drain(mr, m_recv)
 
     end_row = sub == jnp.where(i == 0, 0, 7)
     parts = []
     for b in range(NI):
-        rows = rows_in[b]
+        both = jnp.where(
+            lane % 2 == 0, jnp.where(first_z, zero, rims[0, b]), jnp.where(last_z, zero, rims[1, b])
+        )
+        both = pltpu.roll(both, BZ - 2 * i, 1)
+        corner = jnp.where(
+            lane % 2 == 0, jnp.where(first_z, zero, rims_y[0, b]), jnp.where(last_z, zero, rims_y[1, b])
+        )
+        corner = pltpu.roll(corner, jnp.where(i == 0, BZ - 98, BZ - 96), 1)
+        rows = rows_in[b] + jnp.where(edge, corner, 0.0)
         rows = jnp.where(outside, zero, rows)
         planes = []
         for p in range(PLANES):
+            moved = both if p == 0 else pltpu.roll(both, BZ - 16 * p, 1)
             planes.append(
                 r1[b, p]
+                + jnp.where(edge, moved, 0.0)
                 + jnp.where(end_row, jnp.broadcast_to(rows[p : p + 1], (8, BZ)), 0.0)
             )
         parts.append(planes)
     for b in range(NI):
+        inside = mr[b].astype(F32)
         for a in range(BX):
             value = parts[b][a + 1]
             if a == 0 and b > 0:
@@ -221,7 +240,7 @@
             x = BX * b + a
             sc[x] = value
             cost = CEILING / (1.0 + jnp.exp(-value))
-            xin[x] = jnp.where(mr[b, a] == 1, CEILING, cost)
+            xin[x] = jnp.where(inside[8 * a : 8 * a + 8] > 0.5, CEILING, cost)
 
     acc = xin[...]
     for n in range(1, 32):
@@ -340,6 +359,7 @@
     for after, tk, there in sides:
         @pl.when(there)
         def _():
+            drain(rims_y.at[after, pl.ds(0, 2)], ry_send.at[after])
             drain(rims.at[after], t_send.at[after])
             drain(zb.at[2 * after], r3_send.at[2 * after])
 
@@ -377,9 +397,11 @@
             pltpu.VMEM((5, *tile), F32),
             pltpu.VMEM(tile, F32),
             pltpu.VMEM((NI, PLANES, *tile), F32),
-            pltpu.VMEM((2, *tile), F32),
+            pltpu.VMEM((2, NI, *tile), F32),
+            pltpu.VMEM((2, NI, *tile), F32),
             pltpu.VMEM((NI, *tile), F32),
-            pltpu.VMEM((NI, BX, *tile), jnp.int32),
+            pltpu.VMEM((NI, 32, BZ), jnp.bfloat16),
+            pltpu.VMEM((NI, 32, BZ), jnp.bfloat16),
             pltpu.VMEM((32, *tile), F32),
             pltpu.VMEM((NI, BX, *tile), F32),
             pltpu.VMEM((32, *tile), F32),
@@ -390,7 +412,7 @@
             pltpu.VMEM((3, NJ, BY, BZ), F32),
             pltpu.VMEM((2, 384, BZ), F32),
             dma((3,)),
-        ] + [dma] * 10 + [dma((2,))] * 2 + [dma((3,)), dma((3, 2))],
+        ] + [dma] * 10 + [dma((2,))] * 4 + [dma((3,)), dma((3, 2))],
         compiler_params=pltpu.CompilerParams(
             collective_id=0, has_side_effects=True, vmem_limit_bytes=40 * 1024 * 1024
         ),

time: 31.7 us -> 30.8 us (0.972); the launches traced: 31.2 us -> 30.6 us
  Pallas kernels: 30.5 us -> 30 us
    pallas_call x1, Pallas kernels: 29.7 us -> 29.2 us  [shards(): pl.pallas_call(kernel, out_shape=(out, jax.ShapeDtypeStruct((2, 128, BZ),...]
where the time goes in v6:
time: 30.8 us; the launch traced here: 30.6 us
  Pallas kernels  30 us (97%)
  between operations  0.64 us (2%)
    pallas_call x1, Pallas kernels, shards(): pl.pallas_call(kernel, out_shape=(out, jax.ShapeDtypeStruct((2, 128, BZ),...  29.2 us
    pallas_call x1, Pallas kernels, shards(): pl.pallas_call(finish, out_shape=(out, out), in_specs=[vmem] * 2, out_spe...  0.78 us

profile of v6, /device:TPU:64, one launch (start us, length us, event | category | flops | bytes accessed | tf_op | source)
XLA Modules:
  0.0 30.6 jit_solution(17154697525595623977)
XLA Ops:
  0.6 29.2 %shard_map.50 = (f32[4,64,128]{2,1,0:T(8,128)S(1)}, f32[2,128,128]{2,1,0:T(8,128)S(1)}) custom-call(bf16[32,4,64,128]{3,2,1,0:T(8,128)(2,1)} %f_hbm.1, bf16[27,32]{1,0:T(8,128)(2,1)} %w_hbm.1, s32[4,64,128]{2,1,0:T(8,128)} %m_hbm.1), custom_call_target="tpu_custom_call" | custom-call | tf_op jit(solution)/shard_map/pallas_call | solution.py:385
  29.8 0.8 %shard_map.51 = (f32[4,64,128]{2,1,0:T(8,128)}, f32[4,64,128]{2,1,0:T(8,128)}) custom-call(f32[4,64,128]{2,1,0:T(8,128)S(1)} %get-tuple-element.4.score_in, f32[2,128,128]{2,1,0:T(8,128)S(1)} %get-tuple-element.5.least_ref), custom_call_target="tpu_custom_call" | custom-call | tf_op jit(solution)/shard_map/pallas_call | solution.py:420

commit v7 on v6

--- a/solution.py
+++ b/solution.py
@@ -335,7 +335,7 @@
         later = zb[2, two].reshape(128, BZ).T
         tz[h, 256:384, :] = jnp.where(last_z, FAR, later)
         first = pair // 2
-        for block in range(16):
+        for block in range(8):
             size = 8 * block + 8
 
             def from_before(n, acc):
@@ -348,6 +348,28 @@
             least_ref[first, 0:size, :] = lax.fori_loop(*span, from_before, least_ref[first, 0:size, :], unroll=8)
             rest = slice(128 - size, 128)
             least_ref[first, rest, :] = lax.fori_loop(*span, from_later, least_ref[first, rest, :], unroll=8)
+
+        for block in range(8, 16):
+            size = 8 * block + 8
+            rest = 128 - size
+
+            def from_both(n, parts):
+                square = (n * n).astype(F32)
+                middle = jnp.minimum(
+                    tz[h, pl.ds(128 + rest - n, size - rest), :], tz[h, pl.ds(128 + rest + n, size - rest), :]
+                )
+                found = [jnp.minimum(parts[0], middle + square)]
+                if rest:
+                    found.append(jnp.minimum(parts[1], tz[h, pl.ds(128 - n, rest), :] + square))
+                    found.append(jnp.minimum(parts[2], tz[h, pl.ds(128 + size + n, rest), :] + square))
+                return tuple(found)
+
+            places = [slice(rest, size)] + ([slice(0, rest), slice(size, 128)] if rest else [])
+            found = lax.fori_loop(
+                size - 7, size + 1, from_both, tuple(least_ref[first, place, :] for place in places), unroll=8
+            )
+            for place, value in zip(places, found):
+                least_ref[first, place, :] = value
 
     seven = pl.ds(0, NI - 1)
     drain(mr.at[seven], m_send)

time: 30.8 us -> 30.7 us (level)
  no operation moved by 1% of the time
where the time goes in v7:
time: 30.7 us; the launch traced here: 30.5 us
  Pallas kernels  29.8 us (97%)
  between operations  0.64 us (2%)
    pallas_call x1, Pallas kernels, shards(): pl.pallas_call(kernel, out_shape=(out, jax.ShapeDtypeStruct((2, 128, BZ),...  29.1 us
    pallas_call x1, Pallas kernels, shards(): pl.pallas_call(finish, out_shape=(out, out), in_specs=[vmem] * 2, out_spe...  0.78 us

profile of v7, /device:TPU:64, one launch (start us, length us, event | category | flops | bytes accessed | tf_op | source)
XLA Modules:
  0.0 30.5 jit_solution(10549216696594053611)
XLA Ops:
  0.6 29.1 %shard_map.50 = (f32[4,64,128]{2,1,0:T(8,128)S(1)}, f32[2,128,128]{2,1,0:T(8,128)S(1)}) custom-call(bf16[32,4,64,128]{3,2,1,0:T(8,128)(2,1)} %f_hbm.1, bf16[27,32]{1,0:T(8,128)(2,1)} %w_hbm.1, s32[4,64,128]{2,1,0:T(8,128)} %m_hbm.1), custom_call_target="tpu_custom_call" | custom-call | tf_op jit(solution)/shard_map/pallas_call | solution.py:407
  29.7 0.8 %shard_map.51 = (f32[4,64,128]{2,1,0:T(8,128)}, f32[4,64,128]{2,1,0:T(8,128)}) custom-call(f32[4,64,128]{2,1,0:T(8,128)S(1)} %get-tuple-element.4.score_in, f32[2,128,128]{2,1,0:T(8,128)S(1)} %get-tuple-element.5.least_ref), custom_call_target="tpu_custom_call" | custom-call | tf_op jit(solution)/shard_map/pallas_call | solution.py:442
